TPU v7x, 32 devices: a whole 2x2x4 slice. The times are simulated.
32 devices in a mesh: patch: 8 (over z, x), visit: 4 (over y, core).
Axes of the slice: x: 2, y: 2, z: 4, core: 2. Of those that a mesh axis runs over, the one named last changes fastest.
Arguments:
- template: bfloat16 [8, 1024, 2048], P('patch', 'visit'), may hold values from -40 to 40
- blocks: bfloat16 [1024, 16, 2048], P(('patch', 'visit')), may hold values from -80 to 80
- dest: int32 [1024], P(('patch', 'visit')), may hold values from 0 to 31, as said below
- offset: int32 [1024], P(('patch', 'visit')), may hold values from 0 to 240
- visit_id: int32 [1024], P(('patch', 'visit')), may hold values from 0 to 1
- badmask: int32 [1024, 16], P(('patch', 'visit')), may hold values from 0 to 65535, as said below
Outputs:
- difference: bfloat16 [2, 8, 1024, 2048], P(None, 'patch', 'visit')
- coeffs: float32 [2, 8, 29], P(None, 'patch')
Inputs may be any that keep to these rules, and one draw needn't show every extreme that they name: dest counts devices along patch+visit; of one device's 32 blocks at most 2 go to one device, and one device receives exactly 2 blocks from every device. Bit q of badmask[n, r] flags row r of block n, column group q, as bad.
All inputs are finite; a program needn't handle non-finite values.
Results may differ from a plain program's by a relative error of at most 0.0078.
Values may be sent and summed in bfloat16 or wider, within the bound.
No kernel may reach another device: no remote copies, remote signals or barrier semaphores. Data moves between devices by JAX's collectives and lax.ppermute only.
A program may use at most 256 MiB of HBM per device.

v0:
```python
import jax
import jax.numpy as jnp
import ml_dtypes
import numpy as np
from jax import lax
from jax.experimental import pallas as pl
from jax.experimental.pallas import tpu as pltpu
from jax.sharding import PartitionSpec as P

BLOCK_ROWS = 16
SLOT_CAP = 2
HALF_TAPS = 10
NTAPS = 2 * HALF_TAPS + 1
DEGREE = 6
NPOW = DEGREE + 1
VISITS = 2
BASIS_COUNT = 28
TERMS = 29
GROUPS = 16
TILE = 64
SPAN = 96
SIGMA = 2.0
MIB = 1 << 20


def taps_table():
    places = np.arange(-HALF_TAPS, HALF_TAPS + 1) * 1.0
    basis_rows = []
    for exponent in range(NPOW):
        vector = places**exponent * np.exp(-(places**2) / (2.0 * SIGMA**2))
        for earlier in basis_rows:
            vector = vector - np.dot(earlier, vector) * earlier
        vector = vector / np.sqrt(np.dot(vector, vector))
        basis_rows.append(vector)
    table = np.stack(basis_rows).astype(np.float32)
    return table.astype(ml_dtypes.bfloat16).astype(np.float32)


def band(taps_row, count_out, count_in):
    out = np.zeros((count_out, count_in), np.float32)
    for row in range(count_out):
        out[row, row : row + NTAPS] = taps_row
    return out


def column_table(taps):
    return np.concatenate([band(taps[j], 128, 256).T for j in range(NPOW)], axis=1)


def row_table(taps):
    bands = np.stack([band(taps[i], TILE, SPAN) for i in range(NPOW)])
    bands = bands.reshape(NPOW, TILE // 8, 8, SPAN)
    pieces = []
    for j in range(NPOW):
        pieces.append(bands[: NPOW - j].transpose(1, 0, 2, 3).reshape(-1, SPAN))
    return np.concatenate(pieces, axis=0)


def place_table():
    out = np.zeros((TERMS, 8, 128), np.float32)
    index = 0
    for j in range(NPOW):
        for i in range(NPOW - j):
            out[index, i, j] = 1.0
            index += 1
    out[BASIS_COUNT, 7, 0] = 1.0
    return out


def params(mib):
    return pltpu.CompilerParams(vmem_limit_bytes=mib * MIB)


def pack_kernel(dest, offset, visit, bad_s, bad_v, blocks, send, meta, buf, out, zero, cnt, sem_in, sem_out, row_count):
    count = blocks.shape[0]
    cols = blocks.shape[2]
    slots = send.shape[0]
    group = min(8, count)
    for k in range(count // group):
        part = pl.ds(k * group, group)
        pltpu.make_async_copy(blocks.at[part], buf.at[part], sem_in.at[k]).start()
    zero[...] = jnp.zeros_like(zero)

    def clear(d, carry):
        cnt[d] = 0
        return carry

    lax.fori_loop(0, slots // SLOT_CAP, clear, 0)
    flags = jnp.transpose(bad_v[...])
    for k in range(count // group):
        part = pl.ds(k * group, group)
        pltpu.make_async_copy(blocks.at[part], buf.at[part], sem_in.at[k]).wait()
        for n in range(k * group, (k + 1) * group):
            word = jnp.broadcast_to(flags[:, n : n + 1], (BLOCK_ROWS, 128))
            for q in range(GROUPS):
                lanes = slice(q * (cols // GROUPS), (q + 1) * (cols // GROUPS))
                good = (1 - jnp.bitwise_and(jnp.right_shift(word, q), 1)).astype(jnp.float32)
                out[n, :, lanes] = buf[n, :, lanes] * good.astype(jnp.bfloat16)
            d = dest[n]
            rank = cnt[d]
            cnt[d] = rank + 1
            pltpu.make_async_copy(out.at[n], send.at[d * SLOT_CAP + rank], sem_out).start()

    def fill(d, carry):
        for r in range(SLOT_CAP):

            @pl.when(cnt[d] <= r)
            def _():
                pltpu.make_async_copy(zero, send.at[d * SLOT_CAP + r], sem_out).start()
                meta[d * SLOT_CAP + r, 0] = -1

        cnt[d] = 0
        return carry

    lax.fori_loop(0, slots // SLOT_CAP, fill, 0)

    def describe(n, carry):
        d = dest[n]
        rank = cnt[d]
        cnt[d] = rank + 1
        slot = d * SLOT_CAP + rank
        meta[slot, 0] = visit[n] * row_count + offset[n]
        for r in range(BLOCK_ROWS):
            meta[slot, 1 + r] = bad_s[n, r]
        return carry

    lax.fori_loop(0, count, describe, 0)
    pltpu.make_async_copy(send, send, sem_out).wait()


def pack(dest, offset, visit_id, badmask, blocks, slots, row_count):
    count, _, cols = blocks.shape
    smem = pl.BlockSpec(memory_space=pltpu.SMEM)
    hbm = pl.BlockSpec(memory_space=pl.ANY)

    def kernel(*refs):
        pack_kernel(*refs, row_count=row_count)

    return pl.pallas_call(
        kernel,
        out_shape=(
            jax.ShapeDtypeStruct((slots, BLOCK_ROWS, cols), jnp.bfloat16),
            jax.ShapeDtypeStruct((slots, 1 + BLOCK_ROWS), jnp.int32),
        ),
        in_specs=[smem, smem, smem, smem, pl.BlockSpec(memory_space=pltpu.VMEM), hbm],
        out_specs=(hbm, smem),
        scratch_shapes=[
            pltpu.VMEM((count, BLOCK_ROWS, cols), jnp.bfloat16),
            pltpu.VMEM((count, BLOCK_ROWS, cols), jnp.bfloat16),
            pltpu.VMEM((BLOCK_ROWS, cols), jnp.bfloat16),
            pltpu.SMEM((slots // SLOT_CAP,), jnp.int32),
            pltpu.SemaphoreType.DMA((max(1, count // 8),)),
            pltpu.SemaphoreType.DMA,
        ],
        compiler_params=params(40),
        name="pack_blocks",
    )(dest, offset, visit_id, badmask, badmask, blocks)


def column_kernel(padded, table, out):
    chunk = out.shape[2]
    base = pl.program_id(0) * chunk
    for k in range(chunk // 128):
        start = pl.multiple_of(base + k * 128, 128)
        window = padded[:, pl.ds(start, 256)]
        result = jnp.dot(window, table[...], preferred_element_type=jnp.float32)
        for j in range(NPOW):
            out[j, :, k * 128 : (k + 1) * 128] = result[:, j * 128 : (j + 1) * 128].astype(jnp.bfloat16)


def column_pass(padded, taps, cols):
    rows = padded.shape[0]
    chunk = 512
    table = jnp.asarray(column_table(taps).astype(ml_dtypes.bfloat16))
    return pl.pallas_call(
        column_kernel,
        grid=(cols // chunk,),
        out_shape=jax.ShapeDtypeStruct((NPOW, rows, cols), jnp.bfloat16),
        in_specs=[
            pl.BlockSpec(padded.shape, lambda c: (0, 0)),
            pl.BlockSpec(table.shape, lambda c: (0, 0)),
        ],
        out_specs=pl.BlockSpec((NPOW, rows, chunk), lambda c: (0, 0, c)),
        compiler_params=params(24),
        name="column_pass",
    )(padded, table)


GRAM_ROWS = 240


def gram_kernel(images, table, weight, out, stage):
    cols = images.shape[2]
    chunk = 1024
    step = pl.program_id(0)

    @pl.when(step == 0)
    def _():
        out[...] = jnp.zeros_like(out)

    first = pl.multiple_of(step * TILE, TILE)
    ones = jnp.ones((8, chunk), jnp.float32)
    blank = jnp.zeros((8, chunk), jnp.float32)
    for k in range(cols // chunk):
        lanes = slice(k * chunk, (k + 1) * chunk)
        at = 0
        for j in range(NPOW):
            size = TILE * (NPOW - j)
            window = images[j, pl.ds(first, SPAN), lanes]
            stage[at : at + size, :] = jnp.dot(
                table[at : at + size, :], window, preferred_element_type=jnp.float32
            )
            at += size
        for cb in range(TILE // 8):
            pieces = []
            at = 0
            for j in range(NPOW):
                size = 8 * (NPOW - j)
                pieces.append(stage[at + cb * size : at + (cb + 1) * size, :])
                at += TILE * (NPOW - j)
            basis = jnp.concatenate(pieces + [ones, blank], axis=0)
            scaled = []
            for v in range(VISITS):
                w = weight[v, cb * 8 : (cb + 1) * 8, lanes]
                scaled.append(
                    (basis.reshape(GRAM_ROWS // 8, 8, chunk) * w[None]).reshape(GRAM_ROWS, chunk).astype(jnp.bfloat16)
                )
            out[...] += lax.dot_general(
                jnp.concatenate(scaled, axis=0),
                basis.astype(jnp.bfloat16),
                (((1,), (1,)), ((), ())),
                preferred_element_type=jnp.float32,
            )


def gram(images, weight, taps):
    rows = weight.shape[1]
    cols = weight.shape[2]
    table = jnp.asarray(row_table(taps).astype(ml_dtypes.bfloat16))
    acc = pl.pallas_call(
        gram_kernel,
        grid=(rows // TILE,),
        out_shape=jax.ShapeDtypeStruct((VISITS * GRAM_ROWS, GRAM_ROWS), jnp.float32),
        in_specs=[
            pl.BlockSpec(images.shape, lambda t: (0, 0, 0)),
            pl.BlockSpec(table.shape, lambda t: (0, 0)),
            pl.BlockSpec((VISITS, TILE, cols), lambda t: (0, t, 0)),
        ],
        out_specs=pl.BlockSpec((VISITS * GRAM_ROWS, GRAM_ROWS), lambda t: (0, 0)),
        scratch_shapes=[pltpu.VMEM((BASIS_COUNT * TILE, 1024), jnp.float32)],
        compiler_params=params(48),
        name="gram",
    )(images, table, weight)
    blocks = acc.reshape(VISITS, GRAM_ROWS // 8, 8, GRAM_ROWS // 8, 8)
    same = jnp.asarray(np.eye(8, dtype=np.float32))[None, None, :, None, :]
    return jnp.sum(blocks * same, axis=(2, 4))[:, :TERMS, :TERMS]


def place_kernel(got, placing, count, images, table, science, sums, acc, total):
    step = pl.program_id(0)
    rows = science.shape[1]

    @pl.when(step == 0)
    def _():
        acc[...] = jnp.zeros_like(acc)
        total[...] = jnp.zeros_like(total)

    chunk = science.shape[2]
    summed = jnp.dot(placing[...], got[...].reshape(-1, chunk), preferred_element_type=jnp.float32)
    spread = count[...].astype(jnp.float32)
    value = (summed / jnp.maximum(spread, 1.0)).astype(jnp.bfloat16)
    science[...] = value.reshape(science.shape)
    weighted = value * jnp.minimum(spread, 1.0).astype(jnp.bfloat16)
    for v in range(VISITS):
        part = weighted[v * rows : (v + 1) * rows, :].astype(jnp.float32)
        fold = jnp.sum(part.reshape(rows // 8, 8, chunk), axis=0)
        total[v * 8 : (v + 1) * 8, :] += sum(fold[:, k * 128 : (k + 1) * 128] for k in range(chunk // 128))
    partial = None
    for t in range(rows // TILE):
        left = jnp.concatenate(
            [weighted[v * rows + t * TILE : v * rows + (t + 1) * TILE, :] for v in range(VISITS)], axis=0
        )
        right = images[:, t * TILE : t * TILE + SPAN, :].reshape(NPOW * SPAN, chunk)
        product = lax.dot_general(left, right, (((1,), (1,)), ((), ())), preferred_element_type=jnp.float32)
        partial = product if partial is None else partial + product
    acc[...] += partial

    @pl.when(step == pl.num_programs(0) - 1)
    def _():
        row_id = lax.broadcasted_iota(jnp.int32, (16, 128), 0)
        lane_id = lax.broadcasted_iota(jnp.int32, (16, 128), 1)
        result = jnp.zeros((16, 128), jnp.float32)
        for v in range(VISITS):
            for j in range(NPOW):
                cross = acc[v * TILE : (v + 1) * TILE, j * SPAN : (j + 1) * SPAN]
                for i in range(NPOW - j):
                    item = jnp.sum(cross * table[i], axis=0, keepdims=True)
                    item = jnp.sum(item, axis=1, keepdims=True)
                    result += jnp.where((row_id == v * 8 + i) & (lane_id == j), item, 0.0)
            item = jnp.sum(total[v * 8 : (v + 1) * 8, :], axis=0, keepdims=True)
            item = jnp.sum(item, axis=1, keepdims=True)
            result += jnp.where((row_id == v * 8 + 7) & (lane_id == 0), item, 0.0)
        sums[...] = result


def place(got, placing, count, images, bands, row_count):
    slots, _, cols = got.shape
    chunk = 256
    return pl.pallas_call(
        place_kernel,
        grid=(cols // chunk,),
        out_shape=(
            jax.ShapeDtypeStruct((VISITS, row_count, cols), jnp.bfloat16),
            jax.ShapeDtypeStruct((16, 128), jnp.float32),
        ),
        in_specs=[
            pl.BlockSpec((slots, BLOCK_ROWS, chunk), lambda c: (0, 0, c)),
            pl.BlockSpec(placing.shape, lambda c: (0, 0)),
            pl.BlockSpec((VISITS * row_count, chunk), lambda c: (0, c)),
            pl.BlockSpec((NPOW, images.shape[1], chunk), lambda c: (0, 0, c)),
            pl.BlockSpec(bands.shape, lambda c: (0, 0, 0)),
        ],
        out_specs=(
            pl.BlockSpec((VISITS, row_count, chunk), lambda c: (0, 0, c)),
            pl.BlockSpec((16, 128), lambda c: (0, 0)),
        ),
        scratch_shapes=[
            pltpu.VMEM((VISITS * TILE, NPOW * SPAN), jnp.float32),
            pltpu.VMEM((16, 128), jnp.float32),
        ],
        compiler_params=params(40),
        name="place_and_correlate",
    )(got, placing, count, images, bands)


def model_kernel(sums, inverse, table, images, science, count, out, coeffs, wide, narrow, level):
    step = pl.program_id(0)
    rows = science.shape[1]
    chunk = science.shape[2]

    @pl.when(step == 0)
    def _():
        rhs = sums[0:16, :]
        for k in range(1, sums.shape[0] // 16):
            rhs = rhs + sums[k * 16 : (k + 1) * 16, :]
        row_id = lax.broadcasted_iota(jnp.int32, (32, 128), 0)
        lane_id = lax.broadcasted_iota(jnp.int32, (32, 128), 1)
        for v in range(VISITS):
            product = inverse[v] * rhs[v * 8 : (v + 1) * 8, :][None]
            column = jnp.sum(jnp.sum(product, axis=1), axis=1, keepdims=True)
            row = jnp.sum(jnp.where(row_id == lane_id, column, 0.0), axis=0, keepdims=True)
            coeffs[v : v + 1, :] = row[:, :TERMS]
            level[v * 8 : (v + 1) * 8, :] = jnp.broadcast_to(column[BASIS_COUNT : BASIS_COUNT + 1, :], (8, 128))
            index = 0
            for j in range(NPOW):
                kernel = jnp.zeros((TILE, SPAN), jnp.float32)
                for i in range(NPOW - j):
                    kernel = kernel + column[index : index + 1, :] * table[i]
                    index += 1
                wide[v * TILE : (v + 1) * TILE, j * SPAN : (j + 1) * SPAN] = kernel
        narrow[...] = wide[...].astype(jnp.bfloat16)

    for t in range(rows // TILE):
        right = images[:, t * TILE : t * TILE + SPAN, :].reshape(NPOW * SPAN, chunk)
        model = jnp.dot(narrow[...], right, preferred_element_type=jnp.float32)
        for v in range(VISITS):
            at = slice(t * TILE, (t + 1) * TILE)
            full = model[v * TILE : (v + 1) * TILE, :] + level[v * 8 : v * 8 + 1, 0:1]
            weight = jnp.minimum(count[v, at, :].astype(jnp.float32), 1.0)
            out[v, at, :] = (weight * (science[v, at, :].astype(jnp.float32) - full)).astype(jnp.bfloat16)


def model(sums, inverse, images, science, count, bands):
    _, rows, cols = science.shape
    chunk = 256
    return pl.pallas_call(
        model_kernel,
        grid=(cols // chunk,),
        out_shape=(
            jax.ShapeDtypeStruct((VISITS, rows, cols), jnp.bfloat16),
            jax.ShapeDtypeStruct((VISITS, TERMS), jnp.float32),
        ),
        in_specs=[
            pl.BlockSpec(sums.shape, lambda c: (0, 0)),
            pl.BlockSpec(inverse.shape, lambda c: (0, 0, 0, 0)),
            pl.BlockSpec(bands.shape, lambda c: (0, 0, 0)),
            pl.BlockSpec((NPOW, images.shape[1], chunk), lambda c: (0, 0, c)),
            pl.BlockSpec((VISITS, rows, chunk), lambda c: (0, 0, c)),
            pl.BlockSpec((VISITS, rows, chunk), lambda c: (0, 0, c)),
        ],
        out_specs=(
            pl.BlockSpec((VISITS, rows, chunk), lambda c: (0, 0, c)),
            pl.BlockSpec((VISITS, TERMS), lambda c: (0, 0)),
        ),
        scratch_shapes=[
            pltpu.VMEM((VISITS * TILE, NPOW * SPAN), jnp.float32),
            pltpu.VMEM((VISITS * TILE, NPOW * SPAN), jnp.bfloat16),
            pltpu.VMEM((16, 128), jnp.float32),
        ],
        compiler_params=params(40),
        name="model_and_difference",
    )(sums, inverse, bands, images, science, count)


def inverse_of(matrix):
    eye = jnp.broadcast_to(jnp.eye(TERMS, dtype=jnp.float32), matrix.shape)
    lower = jnp.linalg.cholesky(matrix)
    half = jax.scipy.linalg.solve_triangular(lower, eye, lower=True)
    return jnp.einsum("vkb,vkc->vbc", half, half, precision=lax.Precision.HIGHEST)


def halo(rows):
    count = lax.axis_size("visit")
    up = [(i, i + 1) for i in range(count - 1)]
    down = [(i + 1, i) for i in range(count - 1)]
    above = lax.ppermute(rows[-HALF_TAPS:], "visit", up)
    below = lax.ppermute(rows[:HALF_TAPS], "visit", down)
    return above, below


def coverage(got_meta, row_count):
    slots = got_meta.shape[0]
    start = got_meta[:, 0]
    words = got_meta[:, 1:]
    shifts = jnp.arange(GROUPS, dtype=jnp.int32)[None, None, :]
    bad = jnp.bitwise_and(jnp.right_shift(words[:, :, None], shifts), 1)
    good = (1 - bad).astype(jnp.bfloat16).reshape(slots * BLOCK_ROWS, GROUPS)
    target = jnp.where(
        start[:, None] >= 0,
        start[:, None] + jnp.arange(BLOCK_ROWS, dtype=jnp.int32)[None, :],
        -1,
    ).reshape(-1)
    placing = (jnp.arange(VISITS * row_count, dtype=jnp.int32)[:, None] == target[None, :]).astype(jnp.bfloat16)
    counted = jnp.dot(placing, good, preferred_element_type=jnp.float32)
    return placing, counted


def body(template, blocks, dest, offset, visit_id, badmask):
    row_count = template.shape[1]
    cols = template.shape[2]
    axes = ("patch", "visit")
    sources = lax.axis_size("patch") * lax.axis_size("visit")
    slots = sources * SLOT_CAP
    taps = taps_table()
    bands = jnp.asarray(np.stack([band(taps[i], TILE, SPAN) for i in range(NPOW)]))

    send, meta = pack(dest, offset, visit_id, badmask, blocks, slots, row_count)
    got = lax.all_to_all(send, axes, split_axis=0, concat_axis=0, tiled=True)

    above, below = halo(template[0])
    stored = row_count - TILE + SPAN
    tail = stored - row_count - 2 * HALF_TAPS
    tall = jnp.concatenate([above, template[0], below, jnp.zeros((tail, cols), jnp.bfloat16)], axis=0)
    padded = jnp.pad(tall, ((0, 0), (HALF_TAPS, 128 - HALF_TAPS)))
    images = column_pass(padded, taps, cols)

    meta, images = lax.optimization_barrier((meta, images))
    got_meta = lax.all_to_all(meta, axes, split_axis=0, concat_axis=0, tiled=True)
    placing, counted = coverage(got_meta, row_count)
    spread = jnp.repeat(counted, cols // GROUPS, axis=1)
    weight = jnp.minimum(spread, 1.0).reshape(VISITS, row_count, cols)
    count = spread.astype(jnp.bfloat16)

    normal = lax.psum(gram(images, weight, taps), "visit")
    inverse = jnp.einsum(
        "vcb,bij->vcij", inverse_of(normal), jnp.asarray(place_table()), precision=lax.Precision.HIGHEST
    )
    inverse = jnp.pad(inverse, ((0, 0), (0, 32 - TERMS), (0, 0), (0, 0)))

    science, sums = place(got, placing, count, images, bands, row_count)
    sums = lax.all_gather(sums, "visit", axis=0, tiled=True)
    difference, coeffs = model(sums, inverse, images, science, count.reshape(VISITS, row_count, cols), bands)
    return (difference[:, None], coeffs[:, None])


def solution(mesh):
    in_specs = (
        P("patch", "visit", None),
        P(("patch", "visit"), None, None),
        P(("patch", "visit")),
        P(("patch", "visit")),
        P(("patch", "visit")),
        P(("patch", "visit"), None),
    )
    out_specs = (P(None, "patch", "visit", None), P(None, "patch", None))
    return jax.shard_map(body, mesh=mesh, in_specs=in_specs, out_specs=out_specs, check_vma=False)
```

profile of v0, /device:TPU:0, one launch (start us, length us, event | category | flops | bytes accessed | tf_op | source)
XLA Modules:
  0.0 173.7 jit_solution(13402490806283173258)
XLA Ops:
  2.8 3.0 %collective-permute-start = (bf16[10,2048]{1,0:T(8,128)(2,1)S(1)}, bf16[10,2048]{1,0:T(8,128)(2,1)S(1)}, u32[]{:S(2)}, u32[]{:S(2)}) collective-permute-start(bf16[10,2048]{1,0:T(8,128)(2,1)S(1)} %get-tuple-element.30), channel_id=1, source_target_pairs={{0,1},{1,2},{2,3},{4,5},{5,6},{6,7},{8,9},{9,10},{10,11},{12,13},{... | collective-permute-start | bytes 122888 | tf_op jit(solution)/shard_map/ppermute | solution.py:416
  6.7 1.6 copy-done.4
  10.3 12.3 %pack_blocks.1 = (bf16[64,16,2048]{2,1,0:T(8,128)(2,1)S(1)}, s32[64,17]{1,0:T(8,128)S(1)}) custom-call(s32[32]{0:T(128)S(1)} %copy-done.8, s32[32]{0:T(128)S(1)} %copy-done.9, s32[32]{0:T(128)S(1)} %copy-done.10, s32[32,16]{1,0:T(8,128)S(1)} %copy.62.refs_3_.refs_4_, s32[32,16]{1,0:T(8,128)S(1)} %copy.62.refs_3_.refs_4_, bf16[32,16,2048]{2,1,0:T(8,128)(2,1)S(1)} %copy-done.4), custom_call_target="tpu_custom_call" | custom-call | tf_op jit(solution)/shard_map/pack_blocks/pallas_call | solution.py:139
  24.5 3.8 %column_pass.1.images = bf16[7,288,2048]{2,1,0:T(8,128)(2,1)S(1)} custom-call(bf16[288,2176]{1,0:T(8,128)(2,1)S(1)} %pad.8.padded, bf16[256,896]{1,0:T(8,128)(2,1)S(1)} %copy-done.7), custom_call_target="tpu_custom_call" | custom-call | tf_op jit(solution)/shard_map/column_pass/pallas_call | solution.py:175
  28.3 3.2 %copy-done = bf16[7,288,2048]{2,1,0:T(8,128)(2,1)} copy-done((bf16[7,288,2048]{2,1,0:T(8,128)(2,1)}, bf16[7,288,2048]{2,1,0:T(8,128)(2,1)S(1)}, u32[]{:S(2)}) %copy-start) | copy-done | bytes 8257560
  31.4 14.3 %all_to_all.17 = s32[32,2,17]{2,1,0:T(2,128)S(1)} all-to-all(s32[32,2,17]{2,1,0:T(2,128)S(1)} %bitcast.39), channel_id=1, replica_groups=mesh['patch'=8,'visit'=4] {'patch','visit'}, dimensions={0} | all-to-all | bytes 8704 | tf_op jit(solution)/shard_map/all_to_all | solution.py:458
  45.8 3.8 %all-to-all-start = ((bf16[64,16,2048]{2,1,0:T(8,128)(2,1)}), bf16[64,16,2048]{2,1,0:T(8,128)(2,1)}, u32[]{:S(2)}, u32[]{:S(2)}) async-start(bf16[64,16,2048]{2,1,0:T(8,128)(2,1)} %copy-done.3), calls=%async_computation | async-start | bytes 8388608 | tf_op jit(solution)/shard_map/all_to_all | solution.py:448
  50.7 2.2 %broadcast_in_dim.44 = bf16[512,16,128]{2,1,0:T(8,128)(2,1)} broadcast(bf16[512,16]{1,0:T(8,128)(2,1)S(1)} %copy.64), dimensions={0,1} | broadcast | bytes 2113536 | tf_op jit(solution)/shard_map/broadcast_in_dim | solution.py:460
  53.0 2.8 %convert_element_type.26.count = bf16[2,256,2048]{2,1,0:T(8,128)(2,1)S(1)} reshape(bf16[512,16,128]{2,1,0:T(8,128)(2,1)} %broadcast_in_dim.44) | data formatting | bytes 4194304 | tf_op jit(solution)/shard_map/convert_element_type | solution.py:462
  55.8 3.5 %copy.79 = bf16[64,8,16,128]{3,1,2,0:T(8,128)(2,1)} copy(bf16[64,8,16,128]{3,2,1,0:T(8,128)(2,1)} %bitcast.40) | data formatting | bytes 4194304
  59.4 2.6 %broadcast_in_dim.45 = f32[512,16,128]{2,1,0:T(8,128)} broadcast(f32[512,16]{1,0:T(8,128)S(1)} %copy.65), dimensions={0,1} | broadcast | bytes 4227072 | tf_op jit(solution)/shard_map/broadcast_in_dim | solution.py:460
  62.0 5.0 %min.13.weight = f32[2,256,2048]{2,1,0:T(8,128)} reshape(f32[512,16,128]{2,1,0:T(8,128)} %broadcast_in_dim.45) | data formatting | bytes 8388608 | tf_op jit(solution)/shard_map/min | solution.py:461
  67.0 2.2 %copy-done.1 = f32[2,256,2048]{2,1,0:T(8,128)S(1)} copy-done((f32[2,256,2048]{2,1,0:T(8,128)S(1)}, f32[2,256,2048]{2,1,0:T(8,128)}, u32[]{:S(2)}) %copy-start.1) | copy-done | bytes 4194328
  69.2 34.4 %gram.1 = f32[480,240]{1,0:T(8,128)S(1)} custom-call(bf16[7,288,2048]{2,1,0:T(8,128)(2,1)} %copy-done, bf16[1792,96]{1,0:T(8,128)(2,1)S(1)} %copy-done.6, f32[2,256,2048]{2,1,0:T(8,128)S(1)} %copy-done.1), custom_call_target="tpu_custom_call" | custom-call | tf_op jit(solution)/shard_map/gram/pallas_call | solution.py:240
  103.6 6.0 %reshape.59 = f32[2,30,8,30,8]{4,3,2,1,0:T(8,128)} reshape(f32[480,240]{1,0:T(8,128)S(1)} %gram.1) | data formatting | bytes 921600 | tf_op jit(solution)/shard_map/reshape | solution.py:254
  109.6 4.2 %multiply_reduce_fusion = f32[2,30,30]{2,1,0:T(8,128)S(1)} fusion(f32[2,30,8,30,8]{4,3,2,1,0:T(8,128)} %reshape.59, f32[8,8]{1,0:T(8,128)S(1)} %copy-done.13), kind=kLoop, calls=%fused_computation | loop fusion | flops 228600 | bytes 468256 | tf_op jit(solution)/shard_map/reduce_sum | solution.py:256
  113.9 11.8 %psum.7 = f32[2,29,29]{1,2,0:T(8,128)S(1)} all-reduce(f32[2,29,29]{1,2,0:T(8,128)S(1)} %copy.76), channel_id=1, replica_groups=mesh['patch'=8,'visit'=4] {'visit'}, use_global_device_ids=true, to_apply=%region_1.2 | all-reduce | flops 1682 | bytes 13456 | tf_op jit(solution)/shard_map/psum | solution.py:464
  125.8 5.3 %custom-call.8 = f32[2,29,29]{2,1,0:T(8,128)S(1)} custom-call(f32[2,29,29]{2,1,0:T(8,128)S(1)} %fusion.5), custom_call_target="Cholesky" | custom-call | tf_op jit(solution)/shard_map/jit(cholesky)/cholesky | solution.py:407
  131.4 4.5 %custom-call.9 = f32[2,1,29,29]{2,3,1,0:T(8,128)S(1)} custom-call(f32[2,1,29,29]{3,2,1,0:T(8,128)S(1)} %select_bitcast_fusion), custom_call_target="InvertDiagBlocksLowerTriangular" | custom-call | tf_op jit(solution)/shard_map/jit(_solve_triangular)/vmap()/triangular_solve | solution.py:408
  137.2 6.7 %all-to-all-done.got = bf16[64,16,2048]{2,1,0:T(8,128)(2,1)} async-done(((bf16[64,16,2048]{2,1,0:T(8,128)(2,1)}), bf16[64,16,2048]{2,1,0:T(8,128)(2,1)}, u32[]{:S(2)}, u32[]{:S(2)}) %all-to-all-start) | async-done | bytes 4194336 | tf_op jit(solution)/shard_map/all_to_all | solution.py:448
  144.0 1.7 %copy-done.2 = bf16[64,8,16,128]{3,1,2,0:T(8,128)(2,1)S(1)} copy-done((bf16[64,8,16,128]{3,1,2,0:T(8,128)(2,1)S(1)}, bf16[64,8,16,128]{3,1,2,0:T(8,128)(2,1)}, u32[]{:S(2)}) %copy-start.2) | copy-done | bytes 2097176
  146.8 15.3 %place_and_correlate.1 = (bf16[2,256,2048]{2,1,0:T(8,128)(2,1)S(1)}, f32[16,128]{1,0:T(8,128)S(1)}) custom-call(bf16[64,16,2048]{2,1,0:T(8,128)(2,1)} %all-to-all-done.got, bf16[512,1024]{1,0:T(8,128)(2,1)S(1)} %fusion.1.placing, bf16[512,2048]{1,0:T(8,128)(2,1)S(1)} %bitcast.38, bf16[7,288,2048]{2,1,0:T(8,128)(2,1)} %copy-done, f32[7,64,96]{2,1,0:T(8,128)S(1)} %copy-done.5), custom_call_target="tpu_custom_call" | custom-call | tf_op jit(solution)/shard_map/place_and_correlate/pallas_call | solution.py:309
  162.1 5.2 %all_gather.3.sums = f32[64,128]{1,0:T(8,128)S(1)} all-gather(f32[16,128]{1,0:T(8,128)S(1)} %get-tuple-element.14), channel_id=1, replica_groups=mesh['patch'=8,'visit'=4] {'visit'}, dimensions={0}, use_global_device_ids=true | all-gather | bytes 40960 | tf_op jit(solution)/shard_map/all_gather | solution.py:471
  167.3 6.4 %model_and_difference.1 = (bf16[2,256,2048]{2,1,0:T(8,128)(2,1)}, f32[2,29]{1,0:T(2,128)}) custom-call(f32[64,128]{1,0:T(8,128)S(1)} %all_gather.3.sums, f32[2,32,8,128]{3,2,1,0:T(8,128)S(1)} %pad.9.inverse, f32[7,64,96]{2,1,0:T(8,128)S(1)} %copy-done.5, bf16[7,288,2048]{2,1,0:T(8,128)(2,1)S(1)} %bitcast.37, ...), custom_call_target="tpu_custom_call" | custom-call | tf_op jit(solution)/shard_map/model_and_difference/pallas_call | solution.py:376
  (62 shorter events, 11.0 us)
Async XLA Ops:
  1.5 21.0 %collective-permute-start.1 = (bf16[10,2048]{1,0:T(8,128)(2,1)S(1)}, bf16[10,2048]{1,0:T(8,128)(2,1)S(1)}, u32[]{:S(2)}, u32[]{:S(2)}) collective-permute-start(bf16[10,2048]{1,0:T(8,128)(2,1)S(1)} %get-tuple-element.31), channel_id=1, source_target_pairs={{1,0},{2,1},{3,2},{5,4},{6,5},{7,6},{9,8},{10,9},{11,10},{13,12},{... | collective-permute-start | bytes 122888 | tf_op jit(solution)/shard_map/ppermute | solution.py:417
  2.8 19.7 %collective-permute-start = (bf16[10,2048]{1,0:T(8,128)(2,1)S(1)}, bf16[10,2048]{1,0:T(8,128)(2,1)S(1)}, u32[]{:S(2)}, u32[]{:S(2)}) collective-permute-start(bf16[10,2048]{1,0:T(8,128)(2,1)S(1)} %get-tuple-element.30), channel_id=1, source_target_pairs={{0,1},{1,2},{2,3},{4,5},{5,6},{6,7},{8,9},{9,10},{10,11},{12,13},{... | collective-permute-start | bytes 122888 | tf_op jit(solution)/shard_map/ppermute | solution.py:416
  6.7 1.6 copy-start.4
  8.3 0.7 copy-start.8
  9.0 0.7 copy-start.9
  9.6 0.7 copy-start.10
  10.3 12.3 %copy-start.11 = (bf16[1,256,2048]{2,1,0:T(8,128)(2,1)S(1)}, bf16[1,256,2048]{2,1,0:T(8,128)(2,1)}, u32[]{:S(2)}) copy-start(bf16[1,256,2048]{2,1,0:T(8,128)(2,1)} %param.11) | copy-start | bytes 3145732
  22.5 1.9 %copy-start.3 = (bf16[64,16,2048]{2,1,0:T(8,128)(2,1)}, bf16[64,16,2048]{2,1,0:T(8,128)(2,1)S(1)}, u32[]{:S(2)}) copy-start(bf16[64,16,2048]{2,1,0:T(8,128)(2,1)S(1)} %get-tuple-element.10) | copy-start | bytes 12582916
  22.6 1.9 %copy-start.7 = (bf16[256,896]{1,0:T(8,128)(2,1)S(1)}, bf16[256,896]{1,0:T(8,128)(2,1)}, u32[]{:S(2)}) copy-start(bf16[256,896]{1,0:T(8,128)(2,1)} %constant.70.clone.table) | copy-start | bytes 1376260
  28.3 3.2 %copy-start = (bf16[7,288,2048]{2,1,0:T(8,128)(2,1)}, bf16[7,288,2048]{2,1,0:T(8,128)(2,1)S(1)}, u32[]{:S(2)}) copy-start(bf16[7,288,2048]{2,1,0:T(8,128)(2,1)S(1)} %column_pass.1.images) | copy-start | bytes 24772612
  45.8 98.2 %all-to-all-start = ((bf16[64,16,2048]{2,1,0:T(8,128)(2,1)}), bf16[64,16,2048]{2,1,0:T(8,128)(2,1)}, u32[]{:S(2)}, u32[]{:S(2)}) async-start(bf16[64,16,2048]{2,1,0:T(8,128)(2,1)} %copy-done.3), calls=%async_computation | async-start | bytes 8388608 | tf_op jit(solution)/shard_map/all_to_all | solution.py:448
  62.0 5.0 %copy-start.6 = (bf16[1792,96]{1,0:T(8,128)(2,1)S(1)}, bf16[1792,96]{1,0:T(8,128)(2,1)}, u32[]{:S(2)}) copy-start(bf16[1792,96]{1,0:T(8,128)(2,1)} %constant.71.clone.table) | copy-start | bytes 1032196
  67.0 2.2 %copy-start.1 = (f32[2,256,2048]{2,1,0:T(8,128)S(1)}, f32[2,256,2048]{2,1,0:T(8,128)}, u32[]{:S(2)}) copy-start(f32[2,256,2048]{2,1,0:T(8,128)} %min.13.weight) | copy-start | bytes 12582916
  103.6 6.0 %copy-start.13 = (f32[8,8]{1,0:T(8,128)S(1)}, f32[8,8]{1,0:T(8,128)}, u32[]{:S(2)}) copy-start(f32[8,8]{1,0:T(8,128)} %constant.72.clone) | copy-start | bytes 772
  109.6 26.8 %copy-start.12 = (f32[29,8,128,1]{2,0,1,3:T(8,128)S(1)}, f32[29,8,128,1]{2,0,1,3:T(8,128)}, u32[]{:S(2)}) copy-start(f32[29,8,128,1]{2,0,1,3:T(8,128)} %constant.79) | copy-start | bytes 356356
  144.0 23.3 %slice-start = ((s8[8257536]{0:T(1024)(128)(4,1)}), s8[4194304]{0:T(1024)(128)(4,1)S(1)}, s32[]{:S(2)}) async-start(s8[8257536]{0:T(1024)(128)(4,1)} %bitcast.36), calls=%async_computation.2 | async-start | bytes 8388608
  144.0 1.7 %copy-start.2 = (bf16[64,8,16,128]{3,1,2,0:T(8,128)(2,1)S(1)}, bf16[64,8,16,128]{3,1,2,0:T(8,128)(2,1)}, u32[]{:S(2)}) copy-start(bf16[64,8,16,128]{3,1,2,0:T(8,128)(2,1)} %copy.79) | copy-start | bytes 6291460
  145.7 1.1 copy-start.5
  146.8 20.5 %slice-start.1 = ((s8[8257536]{0:T(1024)(128)(4,1)}), s8[4063232]{0:T(1024)(128)(4,1)S(1)}, s32[]{:S(2)}) async-start(s8[8257536]{0:T(1024)(128)(4,1)} %bitcast.36), calls=%async_computation.3 | async-start | bytes 8126464
where the time goes:
time: 174 us
  Pallas kernels  72.1 us (41%)
  local copies, waits for them, and re-layouts  38 us (22%)
  blocking collectives  31.4 us (18%)
  other arithmetic  15.1 us (9%)
  starting transfers between devices  8.09 us (5%)
  waiting for transfers between devices  6.75 us (4%)
    pallas_call x1, Pallas kernels, gram(): pl.pallas_call(gram_kernel, grid=(rows // TILE,), out_shape=jax.ShapeDtyp...  34.4 us
    unnamed x35, local copies, waits for them, and re-layouts  17.1 us
    pallas_call x1, Pallas kernels, place(): pl.pallas_call(place_kernel, grid=(cols // chunk,), out_shape=(jax.ShapeD...  15.3 us
    all_to_all x1, blocking collectives, body(): lax.all_to_all(meta, axes, split_axis=0, concat_axis=0, tiled=True)  14.3 us
    pallas_call x1, Pallas kernels, pack(): pl.pallas_call(kernel, out_shape=(jax.ShapeDtypeStruct((slots, BLOCK_ROWS...  12.3 us
    psum x1, blocking collectives, body(): normal = lax.psum(gram(images, weight, taps), 'visit')  11.8 us
    all_to_all x1, waiting for transfers between devices, body(): got = lax.all_to_all(send, axes, split_axis=0, concat_axis=0, tiled=True)  6.75 us
    pallas_call x1, Pallas kernels, model(): pl.pallas_call(model_kernel, grid=(cols // chunk,), out_shape=(jax.ShapeD...  6.4 us
  transfers between devices with their start and end apart: 3, of which 1 were waited for; matrix products, arithmetic and copies ran while one was open for 23% of the time, Pallas kernels for 27%

commit v1 on v0

v1 whole, which is shorter than its diff:
```python
import jax
import jax.numpy as jnp
import ml_dtypes
import numpy as np
from jax import lax
from jax.experimental import pallas as pl
from jax.experimental.pallas import tpu as pltpu
from jax.sharding import PartitionSpec as P

BLOCK_ROWS = 16
SLOT_CAP = 2
HALF_TAPS = 10
NTAPS = 2 * HALF_TAPS + 1
DEGREE = 6
NPOW = DEGREE + 1
VISITS = 2
BASIS_COUNT = 28
TERMS = 29
GROUPS = 16
TILE = 64
SPAN = 96
SIGMA = 2.0
MARGIN = 16
MIB = 1 << 20


def taps_table():
    places = np.arange(-HALF_TAPS, HALF_TAPS + 1) * 1.0
    basis_rows = []
    for exponent in range(NPOW):
        vector = places**exponent * np.exp(-(places**2) / (2.0 * SIGMA**2))
        for earlier in basis_rows:
            vector = vector - np.dot(earlier, vector) * earlier
        vector = vector / np.sqrt(np.dot(vector, vector))
        basis_rows.append(vector)
    table = np.stack(basis_rows).astype(np.float32)
    return table.astype(ml_dtypes.bfloat16).astype(np.float32)


def band(taps_row, count_out, count_in, shift=0):
    out = np.zeros((count_out, count_in), np.float32)
    for row in range(count_out):
        out[row, row + shift : row + shift + NTAPS] = taps_row
    return out


def column_table(taps):
    return np.concatenate([band(taps[j], 128, 256).T for j in range(NPOW)], axis=1)


def row_bands(taps):
    return np.stack([band(taps[i], TILE, SPAN, MARGIN - HALF_TAPS) for i in range(NPOW)])


def row_table(taps):
    bands = row_bands(taps)
    bands = bands.reshape(NPOW, TILE // 8, 8, SPAN)
    pieces = []
    for j in range(NPOW):
        pieces.append(bands[: NPOW - j].transpose(1, 0, 2, 3).reshape(-1, SPAN))
    return np.concatenate(pieces, axis=0)


def params(mib):
    return pltpu.CompilerParams(vmem_limit_bytes=mib * MIB)


def describe_kernel(dest, offset, visit, bad, meta, row_count):
    count = dest.shape[1]
    slots = meta.shape[0]
    goal = jnp.broadcast_to(dest[...].astype(jnp.float32), (count, count))
    earlier = lax.broadcasted_iota(jnp.int32, (count, count), 0) < lax.broadcasted_iota(jnp.int32, (count, count), 1)
    rank = jnp.sum(jnp.where((jnp.transpose(goal) == goal) & earlier, 1.0, 0.0), axis=0, keepdims=True)
    slot = goal[0:1, :] * SLOT_CAP + rank
    own = lax.broadcasted_iota(jnp.int32, (slots, count), 0).astype(jnp.float32) == slot
    pick = jnp.where(own, 1.0, 0.0)
    start = (visit[...] * row_count + offset[...] + 1).astype(jnp.float32)
    landing = jnp.sum(jnp.where(own, start, 0.0), axis=1, keepdims=True) - 1.0
    words = lax.dot_general(
        pick,
        bad[...].astype(jnp.float32),
        (((1,), (1,)), ((), ())),
        precision=lax.Precision.HIGHEST,
        preferred_element_type=jnp.float32,
    )
    meta[:, 0:BLOCK_ROWS] = words.astype(jnp.int32)
    meta[:, BLOCK_ROWS : BLOCK_ROWS + 1] = landing.astype(jnp.int32)


def describe(dest, offset, visit_id, flags, slots, row_count):
    vmem = pl.BlockSpec(memory_space=pltpu.VMEM)

    def kernel(*refs):
        describe_kernel(*refs, row_count=row_count)

    return pl.pallas_call(
        kernel,
        out_shape=jax.ShapeDtypeStruct((slots, 1 + BLOCK_ROWS), jnp.int32),
        in_specs=[vmem] * 4,
        out_specs=vmem,
        name="describe_blocks",
    )(dest[None, :], offset[None, :], visit_id[None, :], flags)


def pack_kernel(dest_hbm, bad_hbm, blocks, send, dest, bad, buf, out, zero, spread, cnt, where, sem_small, sem_in, sem_out):
    count = blocks.shape[0]
    cols = blocks.shape[2]
    slots = send.shape[0]
    group = min(8, count)
    small = [
        pltpu.make_async_copy(dest_hbm, dest, sem_small.at[0]),
        pltpu.make_async_copy(bad_hbm, bad, sem_small.at[1]),
    ]
    for item in small:
        item.start()
    for k in range(count // group):
        part = pl.ds(k * group, group)
        pltpu.make_async_copy(blocks.at[part], buf.at[part], sem_in.at[k]).start()

    def reset(d, carry):
        cnt[d] = 0
        return carry

    def locate(n, carry):
        d = dest[n]
        rank = cnt[d]
        cnt[d] = rank + 1
        where[n] = d * SLOT_CAP + rank
        return carry

    def blank(d, carry):
        for r in range(SLOT_CAP):

            @pl.when(cnt[d] <= r)
            def _():
                pltpu.make_async_copy(zero, send.at[d * SLOT_CAP + r], sem_out).start()

        return carry

    zero[...] = jnp.zeros_like(zero)
    lax.fori_loop(0, slots // SLOT_CAP, reset, 0, unroll=8)
    for item in small:
        item.wait()
    lax.fori_loop(0, count, locate, 0, unroll=4)
    lax.fori_loop(0, slots // SLOT_CAP, blank, 0, unroll=4)
    row_id = lax.broadcasted_iota(jnp.int32, (128, 128), 0)
    for q in range(cols // 128):
        spread[:, q * 128 : (q + 1) * 128] = jnp.where(row_id == q * GROUPS // (cols // 128), 1.0, 0.0).astype(jnp.bfloat16)
    flags = bad[...]
    lane = lax.broadcasted_iota(jnp.int32, (BLOCK_ROWS, 128), 1)
    shift = jnp.minimum(lane, GROUPS)
    for k in range(count // group):
        rows = []
        for n in range(k * group, (k + 1) * group):
            word = jnp.broadcast_to(flags[:, n : n + 1], (BLOCK_ROWS, 128))
            bit = jnp.bitwise_and(jnp.right_shift(word, shift), 1)
            rows.append((1 - bit).astype(jnp.float32))
        good = jnp.concatenate(rows, axis=0).astype(jnp.bfloat16)
        mask = jnp.dot(good, spread[...], preferred_element_type=jnp.float32).astype(jnp.bfloat16)
        part = pl.ds(k * group, group)
        pltpu.make_async_copy(blocks.at[part], buf.at[part], sem_in.at[k]).wait()
        out[part] = buf[part] * mask.reshape(group, BLOCK_ROWS, cols)
        for n in range(k * group, (k + 1) * group):
            pltpu.make_async_copy(out.at[n], send.at[where[n]], sem_out).start()
    pltpu.make_async_copy(send, send, sem_out).wait()


def pack(dest, flags, blocks, slots):
    count, _, cols = blocks.shape
    hbm = pl.BlockSpec(memory_space=pltpu.HBM)
    return pl.pallas_call(
        pack_kernel,
        out_shape=pltpu.HBM((slots, BLOCK_ROWS, cols), jnp.bfloat16),
        in_specs=[hbm, hbm, hbm],
        out_specs=hbm,
        scratch_shapes=[
            pltpu.SMEM((count,), jnp.int32),
            pltpu.VMEM((BLOCK_ROWS, count), jnp.int32),
            pltpu.VMEM((count, BLOCK_ROWS, cols), jnp.bfloat16),
            pltpu.VMEM((count, BLOCK_ROWS, cols), jnp.bfloat16),
            pltpu.VMEM((BLOCK_ROWS, cols), jnp.bfloat16),
            pltpu.VMEM((128, cols), jnp.bfloat16),
            pltpu.SMEM((slots // SLOT_CAP,), jnp.int32),
            pltpu.SMEM((count,), jnp.int32),
            pltpu.SemaphoreType.DMA((2,)),
            pltpu.SemaphoreType.DMA((max(1, count // 8),)),
            pltpu.SemaphoreType.DMA,
        ],
        compiler_params=params(24),
        name="pack_blocks",
    )(*(pltpu.with_memory_space_constraint(item, pltpu.HBM) for item in (dest, flags, blocks)))


def cover_kernel(meta, placing, spread):
    slots = meta.shape[0]
    cols = spread.shape[1]
    lines = placing.shape[1]
    rows = placing.shape[0]
    words = jnp.transpose(meta[...].astype(jnp.float32))
    slot_id = lax.broadcasted_iota(jnp.int32, (slots, lines), 0)
    line_id = lax.broadcasted_iota(jnp.int32, (slots, lines), 1)
    pick = jnp.where(slot_id == line_id // BLOCK_ROWS, 1.0, 0.0).astype(jnp.float32)
    wide = jnp.dot(words, pick, precision=lax.Precision.HIGHEST, preferred_element_type=jnp.float32)
    lane = lax.broadcasted_iota(jnp.int32, (1, lines), 1)
    inner = lane % BLOCK_ROWS
    start = wide[BLOCK_ROWS : BLOCK_ROWS + 1, :].astype(jnp.int32)
    target = jnp.where(start >= 0, start + inner, -1)
    own = lax.broadcasted_iota(jnp.int32, (BLOCK_ROWS, lines), 0) == inner
    word = jnp.sum(jnp.where(own, wide[0:BLOCK_ROWS, :], 0.0), axis=0, keepdims=True).astype(jnp.int32)
    group = lax.broadcasted_iota(jnp.int32, (128, lines), 0)
    bit = jnp.bitwise_and(jnp.right_shift(jnp.broadcast_to(word, (128, lines)), jnp.minimum(group, GROUPS)), 1)
    good = (1 - bit).astype(jnp.float32).astype(jnp.bfloat16)
    step = 128
    for k in range(rows // step):
        row = lax.broadcasted_iota(jnp.int32, (step, lines), 0) + k * step
        placing[k * step : (k + 1) * step, :] = jnp.where(row == target, 1.0, 0.0).astype(jnp.bfloat16)
    counted = lax.dot_general(placing[...], good, (((1,), (1,)), ((), ())), preferred_element_type=jnp.float32)
    wide_group = cols // GROUPS
    for q in range(GROUPS):
        spread[:, q * wide_group : (q + 1) * wide_group] = jnp.broadcast_to(
            counted[:, q : q + 1], (rows, wide_group)
        ).astype(jnp.bfloat16)


def cover(got_meta, row_count, cols):
    slots = got_meta.shape[0]
    vmem = pl.BlockSpec(memory_space=pltpu.VMEM)
    return pl.pallas_call(
        cover_kernel,
        out_shape=(
            jax.ShapeDtypeStruct((VISITS * row_count, slots * BLOCK_ROWS), jnp.bfloat16),
            jax.ShapeDtypeStruct((VISITS * row_count, cols), jnp.bfloat16),
        ),
        in_specs=[vmem],
        out_specs=(vmem, vmem),
        compiler_params=params(24),
        name="coverage",
    )(got_meta)


def column_kernel(padded, table, out):
    for k in range(out.shape[2] // 128):
        window = padded[:, k * 128 : k * 128 + 256]
        result = jnp.dot(window, table[...], preferred_element_type=jnp.float32)
        for j in range(NPOW):
            out[j, :, k * 128 : (k + 1) * 128] = result[:, j * 128 : (j + 1) * 128].astype(jnp.bfloat16)


def column_pass(padded, taps, cols):
    rows = padded.shape[0]
    vmem = pl.BlockSpec(memory_space=pltpu.VMEM)
    table = jnp.asarray(column_table(taps).astype(ml_dtypes.bfloat16))
    return pl.pallas_call(
        column_kernel,
        out_shape=jax.ShapeDtypeStruct((NPOW, rows, cols), jnp.bfloat16),
        in_specs=[vmem, vmem],
        out_specs=vmem,
        compiler_params=params(24),
        name="column_pass",
    )(padded, table)


GRAM_ROWS = 240


def gram_kernel(images, table, count, out, stage, acc):
    cols = images.shape[2]
    rows = count.shape[0] // VISITS
    chunk = stage.shape[1]
    ones = jnp.ones((8, chunk), jnp.float32)
    blank = jnp.zeros((8, chunk), jnp.float32)
    acc[...] = jnp.zeros_like(acc)

    def tile(step, carry):
        first = pl.multiple_of(step * TILE, TILE)
        for k in range(cols // chunk):
            lanes = slice(k * chunk, (k + 1) * chunk)
            at = 0
            for j in range(NPOW):
                size = TILE * (NPOW - j)
                window = images[j, pl.ds(first, SPAN), lanes]
                stage[at : at + size, :] = jnp.dot(
                    table[at : at + size, :], window, preferred_element_type=jnp.float32
                )
                at += size
            for pair in range(TILE // 16):
                seen = [
                    jnp.minimum(
                        count[pl.ds(pl.multiple_of(v * rows + first + pair * 16, 16), 16), lanes].astype(jnp.float32), 1.0
                    )
                    for v in range(VISITS)
                ]
                for half in range(2):
                    cb = pair * 2 + half
                    pieces = []
                    at = 0
                    for j in range(NPOW):
                        size = 8 * (NPOW - j)
                        pieces.append(stage[at + cb * size : at + (cb + 1) * size, :])
                        at += TILE * (NPOW - j)
                    basis = jnp.concatenate(pieces + [ones, blank], axis=0)
                    scaled = []
                    for v in range(VISITS):
                        w = seen[v][half * 8 : half * 8 + 8]
                        scaled.append(
                            (basis.reshape(GRAM_ROWS // 8, 8, chunk) * w[None])
                            .reshape(GRAM_ROWS, chunk)
                            .astype(jnp.bfloat16)
                        )
                    acc[...] += lax.dot_general(
                        jnp.concatenate(scaled, axis=0),
                        basis.astype(jnp.bfloat16),
                        (((1,), (1,)), ((), ())),
                        preferred_element_type=jnp.float32,
                    )
        return carry

    lax.fori_loop(0, rows // TILE, tile, 0)
    row_id = lax.broadcasted_iota(jnp.int32, (GRAM_ROWS, GRAM_ROWS), 0)
    lane_id = lax.broadcasted_iota(jnp.int32, (GRAM_ROWS, GRAM_ROWS), 1)
    same = (row_id % 8) == (lane_id % 8)
    gather = jnp.where(
        lax.broadcasted_iota(jnp.int32, (GRAM_ROWS, 128), 0) // 8
        == lax.broadcasted_iota(jnp.int32, (GRAM_ROWS, 128), 1),
        1.0,
        0.0,
    )
    for v in range(VISITS):
        kept = jnp.where(same, acc[v * GRAM_ROWS : (v + 1) * GRAM_ROWS, :], 0.0)
        kept = jnp.sum(kept.reshape(GRAM_ROWS // 8, 8, GRAM_ROWS), axis=1)
        full = jnp.dot(kept, gather, precision=lax.Precision.HIGHEST, preferred_element_type=jnp.float32)
        out[v] = full[:TERMS, :TERMS]


def gram(images, count, taps):
    vmem = pl.BlockSpec(memory_space=pltpu.VMEM)
    table = jnp.asarray(row_table(taps).astype(ml_dtypes.bfloat16))
    return pl.pallas_call(
        gram_kernel,
        out_shape=jax.ShapeDtypeStruct((VISITS, TERMS, TERMS), jnp.float32),
        in_specs=[vmem, vmem, vmem],
        out_specs=vmem,
        scratch_shapes=[
            pltpu.VMEM((BASIS_COUNT * TILE, 1024), jnp.float32),
            pltpu.VMEM((VISITS * GRAM_ROWS, GRAM_ROWS), jnp.float32),
        ],
        compiler_params=params(28),
        name="normal_matrix",
    )(images, table, count)


def place_kernel(got, placing, count, source, table, science, sums, images, buf, acc, sem_got, sem_img):
    rows = science.shape[1]
    cols = science.shape[2]
    chunk = 256
    copies = []
    for c in range(cols // chunk):
        lanes = slice(c * chunk, (c + 1) * chunk)
        copies.append(
            (
                pltpu.make_async_copy(got.at[:, :, lanes], buf.at[:, :, lanes], sem_got.at[c]),
                pltpu.make_async_copy(source.at[:, :, lanes], images.at[:, :, lanes], sem_img.at[c]),
            )
        )
        for item in copies[-1]:
            item.start()
    partial = None
    total = [jnp.zeros((8, 128), jnp.float32) for _ in range(VISITS)]
    for c in range(cols // chunk):
        lanes = slice(c * chunk, (c + 1) * chunk)
        copies[c][0].wait()
        summed = jnp.dot(placing[...], buf[:, :, lanes].reshape(-1, chunk), preferred_element_type=jnp.float32)
        spread = count[:, lanes].astype(jnp.float32)
        value = (summed / jnp.maximum(spread, 1.0)).astype(jnp.bfloat16)
        weighted = value * jnp.minimum(spread, 1.0).astype(jnp.bfloat16)
        for v in range(VISITS):
            science[v, :, lanes] = value[v * rows : (v + 1) * rows, :]
            part = weighted[v * rows : (v + 1) * rows, :].astype(jnp.float32)
            fold = jnp.sum(part.reshape(rows // 8, 8, chunk), axis=0)
            for k in range(chunk // 128):
                total[v] = total[v] + fold[:, k * 128 : (k + 1) * 128]
        copies[c][1].wait()
        for t in range(rows // TILE):
            left = jnp.concatenate(
                [weighted[v * rows + t * TILE : v * rows + (t + 1) * TILE, :] for v in range(VISITS)], axis=0
            )
            right = images[:, t * TILE : t * TILE + SPAN, lanes].reshape(NPOW * SPAN, chunk)
            product = lax.dot_general(left, right, (((1,), (1,)), ((), ())), preferred_element_type=jnp.float32)
            partial = product if partial is None else partial + product
    acc[...] = partial
    row_id = lax.broadcasted_iota(jnp.int32, (32, 128), 0)
    lane_id = lax.broadcasted_iota(jnp.int32, (32, 128), 1)
    result = jnp.zeros((32, 128), jnp.float32)
    for v in range(VISITS):
        parts = []
        for j in range(NPOW):
            cross = acc[v * TILE : (v + 1) * TILE, j * SPAN : (j + 1) * SPAN]
            for i in range(NPOW - j):
                parts.append(jnp.sum(cross * table[i], axis=0, keepdims=True))
        parts.append(jnp.zeros((32 - BASIS_COUNT, SPAN), jnp.float32))
        item = jnp.sum(jnp.concatenate(parts, axis=0), axis=1, keepdims=True)
        flat = jnp.sum(jnp.sum(total[v], axis=0, keepdims=True), axis=1, keepdims=True)
        item = jnp.where(row_id == BASIS_COUNT, flat, item)
        result = result + jnp.where(lane_id == v, item, 0.0)
    sums[...] = result


def place(got, placing, count, images, bands, row_count):
    slots, _, cols = got.shape
    chunks = cols // 256
    table = jnp.asarray(bands)
    vmem = pl.BlockSpec(memory_space=pltpu.VMEM)
    hbm = pl.BlockSpec(memory_space=pltpu.HBM)
    return pl.pallas_call(
        place_kernel,
        out_shape=(
            jax.ShapeDtypeStruct((VISITS, row_count, cols), jnp.bfloat16),
            jax.ShapeDtypeStruct((32, 128), jnp.float32),
            jax.ShapeDtypeStruct(images.shape, jnp.bfloat16),
        ),
        in_specs=[hbm, vmem, vmem, hbm, vmem],
        out_specs=(vmem, vmem, vmem),
        scratch_shapes=[
            pltpu.VMEM(got.shape, jnp.bfloat16),
            pltpu.VMEM((VISITS * TILE, NPOW * SPAN), jnp.float32),
            pltpu.SemaphoreType.DMA((chunks,)),
            pltpu.SemaphoreType.DMA((chunks,)),
        ],
        compiler_params=params(40),
        name="place_and_correlate",
    )(
        pltpu.with_memory_space_constraint(got, pltpu.HBM),
        placing,
        count,
        pltpu.with_memory_space_constraint(images, pltpu.HBM),
        table,
    )


def model_kernel(sums, inverse, table, images, science, count, out, coeffs, wide, narrow, buf, sem):
    rows = science.shape[1]
    cols = science.shape[2]
    chunk = 256
    rhs = sums[0:32, :]
    for k in range(1, sums.shape[0] // 32):
        rhs = rhs + sums[k * 32 : (k + 1) * 32, :]
    level = []
    for v in range(VISITS):
        row = jnp.sum(inverse[v] * rhs[:, v : v + 1], axis=0, keepdims=True)
        coeffs[v : v + 1, :] = row[:, :TERMS]
        level.append(row[:, BASIS_COUNT : BASIS_COUNT + 1])
        index = 0
        for j in range(NPOW):
            kernel = jnp.zeros((TILE, SPAN), jnp.float32)
            for i in range(NPOW - j):
                kernel = kernel + row[:, index : index + 1] * table[i]
                index += 1
            wide[v * TILE : (v + 1) * TILE, j * SPAN : (j + 1) * SPAN] = kernel
    narrow[...] = wide[...].astype(jnp.bfloat16)
    copies = []
    for c in range(cols // chunk):
        lanes = slice(c * chunk, (c + 1) * chunk)
        for t in range(rows // TILE):
            right = images[:, t * TILE : t * TILE + SPAN, lanes].reshape(NPOW * SPAN, chunk)
            model = jnp.dot(narrow[...], right, preferred_element_type=jnp.float32)
            for v in range(VISITS):
                at = slice(t * TILE, (t + 1) * TILE)
                full = model[v * TILE : (v + 1) * TILE, :] + level[v]
                seen = count[v * rows + t * TILE : v * rows + (t + 1) * TILE, lanes]
                weight = jnp.minimum(seen.astype(jnp.float32), 1.0)
                buf[v, at, lanes] = (weight * (science[v, at, lanes].astype(jnp.float32) - full)).astype(jnp.bfloat16)
        copies.append(pltpu.make_async_copy(buf.at[:, :, lanes], out.at[:, :, lanes], sem.at[c]))
        copies[-1].start()
    for item in copies:
        item.wait()


def model(sums, inverse, images, science, count, bands):
    _, rows, cols = science.shape
    table = jnp.asarray(bands)
    vmem = pl.BlockSpec(memory_space=pltpu.VMEM)
    return pl.pallas_call(
        model_kernel,
        out_shape=(
            pltpu.HBM((VISITS, rows, cols), jnp.bfloat16),
            jax.ShapeDtypeStruct((VISITS, TERMS), jnp.float32),
        ),
        in_specs=[vmem] * 6,
        out_specs=(pl.BlockSpec(memory_space=pltpu.HBM), vmem),
        scratch_shapes=[
            pltpu.VMEM((VISITS * TILE, NPOW * SPAN), jnp.float32),
            pltpu.VMEM((VISITS * TILE, NPOW * SPAN), jnp.bfloat16),
            pltpu.VMEM((VISITS, rows, cols), jnp.bfloat16),
            pltpu.SemaphoreType.DMA((cols // 256,)),
        ],
        compiler_params=params(28),
        name="model_and_difference",
    )(sums, inverse, table, images, science, count)


def inverse_of(matrix):
    eye = jnp.broadcast_to(jnp.eye(TERMS, dtype=jnp.float32), matrix.shape)
    lower = jnp.linalg.cholesky(matrix)
    half = jax.scipy.linalg.solve_triangular(lower, eye, lower=True)
    return jnp.einsum("vkb,vkc->vbc", half, half, precision=lax.Precision.HIGHEST)


def halo(rows):
    count = lax.axis_size("visit")
    up = [(i, i + 1) for i in range(count - 1)]
    down = [(i + 1, i) for i in range(count - 1)]
    above = lax.ppermute(rows[-MARGIN:], "visit", up)
    below = lax.ppermute(rows[:MARGIN], "visit", down)
    return above, below


def body(template, blocks, dest, offset, visit_id, badmask):
    row_count = template.shape[1]
    cols = template.shape[2]
    axes = ("patch", "visit")
    sources = lax.axis_size("patch") * lax.axis_size("visit")
    slots = sources * SLOT_CAP
    taps = taps_table()
    bands = row_bands(taps)

    flags = badmask.T
    meta = describe(dest, offset, visit_id, flags, slots, row_count)
    got_meta = lax.all_to_all(meta, axes, split_axis=0, concat_axis=0, tiled=True)
    send = pack(dest, flags, blocks, slots)
    send, got_meta, rows = lax.optimization_barrier((send, got_meta, template[0]))
    got = lax.all_to_all(send, axes, split_axis=0, concat_axis=0, tiled=True)

    above, below = halo(rows)
    tall = jnp.concatenate([above, rows, below], axis=0)
    padded = jnp.pad(tall, ((0, 0), (HALF_TAPS, 128 - HALF_TAPS)))
    images = column_pass(padded, taps, cols)
    placing, count = cover(got_meta, row_count, cols)

    normal = lax.psum(gram(images, count, taps), "visit")
    inverse = jnp.pad(inverse_of(normal), ((0, 0), (0, 32 - TERMS), (0, 128 - TERMS)))

    science, sums, images = place(got, placing, count, images, bands, row_count)
    sums = lax.all_gather(sums, "visit", axis=0, tiled=True)
    difference, coeffs = model(sums, inverse, images, science, count, bands)
    return (difference[:, None], coeffs[:, None])


def solution(mesh):
    in_specs = (
        P("patch", "visit", None),
        P(("patch", "visit"), None, None),
        P(("patch", "visit")),
        P(("patch", "visit")),
        P(("patch", "visit")),
        P(("patch", "visit"), None),
    )
    out_specs = (P(None, "patch", "visit", None), P(None, "patch", None))
    return jax.shard_map(body, mesh=mesh, in_specs=in_specs, out_specs=out_specs, check_vma=False)
```

time: 174 us -> 138 us (0.79)
  local copies, waits for them, and re-layouts: 38 us -> 4.35 us
  Pallas kernels: 72.1 us -> 57.8 us
  starting transfers between devices: 8.09 us -> 15.2 us
  waiting for transfers between devices: 6.75 us -> 11 us
  blocking collectives: 31.4 us -> 35.5 us
  other arithmetic: 15.1 us -> 11.8 us
    psum x1, blocking collectives: 11.8 us -> 30.3 us  [body(): normal = lax.psum(gram(images, count, taps), 'visit')]
    all_to_all x1 -> x0, blocking collectives: 14.3 us -> none  [body(): lax.all_to_all(meta, axes, split_axis=0, concat_axis=0, tiled=True)]
    pallas_call x5 -> x7, Pallas kernels: 72.1 us -> 57.8 us  [the longest x1 31.3 us: gram(): pl.pallas_call(gram_kernel, out_shape=jax.ShapeDtypeStruct((VISITS, TERMS...]
    unnamed x35 -> x8, local copies, waits for them, and re-layouts: 17.1 us -> 3.2 us
    all_to_all x0 -> x1, starting transfers between devices: none -> 7.3 us  [body(): lax.all_to_all(meta, axes, split_axis=0, concat_axis=0, tiled=True)]
    reshape x1 -> x0, local copies, waits for them, and re-layouts: 5.99 us -> none  [gram(): blocks = acc.reshape(VISITS, GRAM_ROWS // 8, 8, GRAM_ROWS // 8, 8)]
    min x2 -> x0, local copies, waits for them, and re-layouts: 5.12 us -> none  [body(): weight = jnp.minimum(spread, 1.0).reshape(VISITS, row_count, cols)]
    broadcast_in_dim x3 -> x0, local copies, waits for them, and re-layouts: 4.86 us -> none  [the longest x2 4.86 us: body(): spread = jnp.repeat(counted, cols // GROUPS, axis=1)]
  transfers between devices with their start and end apart: 3 -> 4, of which waited for: 1 -> 2; matrix products, arithmetic and copies ran while one was open for 23% -> 10% of each run, Pallas kernels for 27% -> 29%
where the time goes in v1:
time: 138 us; the launch traced here: 137 us
  Pallas kernels  57.8 us (42%)
  blocking collectives  35.5 us (26%)
  starting transfers between devices  15.2 us (11%)
  other arithmetic  11.8 us (9%)
  waiting for transfers between devices  11 us (8%)
  local copies, waits for them, and re-layouts  4.35 us (3%)
    pallas_call x1, Pallas kernels, gram(): pl.pallas_call(gram_kernel, out_shape=jax.ShapeDtypeStruct((VISITS, TERMS...  31.3 us
    psum x1, blocking collectives, body(): normal = lax.psum(gram(images, count, taps), 'visit')  30.3 us
    pallas_call x1, Pallas kernels, place(): pl.pallas_call(place_kernel, out_shape=(jax.ShapeDtypeStruct((VISITS, row...  13 us
    all_to_all x1, waiting for transfers between devices, body(): got = lax.all_to_all(send, axes, split_axis=0, concat_axis=0, tiled=True)  7.55 us
    all_to_all x1, starting transfers between devices, body(): lax.all_to_all(meta, axes, split_axis=0, concat_axis=0, tiled=True)  7.3 us
    another operation x4, other arithmetic, inverse_of(): lower = jnp.linalg.cholesky(matrix)  5.47 us
    all_gather x1, blocking collectives, body(): sums = lax.all_gather(sums, 'visit', axis=0, tiled=True)  5.25 us
    another operation x3, other arithmetic, inverse_of(): half = jax.scipy.linalg.solve_triangular(lower, eye, lower=True)  4.54 us
  transfers between devices with their start and end apart: 4, of which 2 were waited for; matrix products, arithmetic and copies ran while one was open for 10% of the time, Pallas kernels for 29%

profile of v1, /device:TPU:0, one launch (start us, length us, event | category | flops | bytes accessed | tf_op | source)
XLA Modules:
  0.0 137.1 jit_solution(14667339651444282080)
XLA Ops:
  0.6 1.6 %describe_blocks.1 = s32[64,17]{1,0:T(8,128)} custom-call(s32[1,32]{1,0:T(1,128)} %bitcast.30, s32[1,32]{1,0:T(1,128)} %bitcast.31, s32[1,32]{1,0:T(1,128)} %bitcast.32, s32[16,32]{1,0:T(8,128)} %bitcast.28), custom_call_target="tpu_custom_call" | custom-call | tf_op jit(solution)/shard_map/describe_blocks/pallas_call | solution.py:96
  2.2 7.3 %all-to-all-start = ((s32[32,2,17]{2,1,0:T(2,128)}), s32[32,2,17]{2,1,0:T(2,128)S(1)}, u32[]{:S(2)}, u32[]{:S(2)}) async-start(s32[32,2,17]{2,1,0:T(2,128)} %bitcast.27), calls=%async_computation | async-start | bytes 65536 | tf_op jit(solution)/shard_map/all_to_all | solution.py:528
  9.5 3.8 %pack_blocks.1 = bf16[64,16,2048]{2,1,0:T(8,128)(2,1)} custom-call(s32[32]{0:T(128)} %dest_hbm.1, s32[16,32]{1,0:T(8,128)} %bitcast.29, bf16[32,16,2048]{2,1,0:T(8,128)(2,1)} %blocks.1), custom_call_target="tpu_custom_call" | custom-call | tf_op jit(solution)/shard_map/pack_blocks/pallas_call | solution.py:171
  13.3 3.5 %all-to-all-done = s32[32,2,17]{2,1,0:T(2,128)S(1)} async-done(((s32[32,2,17]{2,1,0:T(2,128)}), s32[32,2,17]{2,1,0:T(2,128)S(1)}, u32[]{:S(2)}, u32[]{:S(2)}) %all-to-all-start) | async-done | bytes 4384 | tf_op jit(solution)/shard_map/all_to_all | solution.py:528
  16.8 3.6 %all-to-all-start.1 = ((bf16[64,16,2048]{2,1,0:T(8,128)(2,1)}), bf16[64,16,2048]{2,1,0:T(8,128)(2,1)}, u32[]{:S(2)}, u32[]{:S(2)}) async-start(bf16[64,16,2048]{2,1,0:T(8,128)(2,1)} %pack_blocks.1), calls=%async_computation.1 | async-start | bytes 8388608 | tf_op jit(solution)/shard_map/all_to_all | solution.py:531
  20.4 0.9 fusion.11
  21.4 1.3 collective-permute-start.1
  22.7 3.0 %collective-permute-start = (bf16[16,2048]{1,0:T(8,128)(2,1)S(1)}, bf16[16,2048]{1,0:T(8,128)(2,1)S(1)}, u32[]{:S(2)}, u32[]{:S(2)}) collective-permute-start(bf16[16,2048]{1,0:T(8,128)(2,1)S(1)} %get-tuple-element.26), channel_id=1, source_target_pairs={{0,1},{1,2},{2,3},{4,5},{5,6},{6,7},{8,9},{9,10},{10,11},{12,13},{... | collective-permute-start | bytes 196616 | tf_op jit(solution)/shard_map/ppermute | solution.py:512
  25.7 1.4 %coverage.1 = (bf16[512,1024]{1,0:T(8,128)(2,1)S(1)}, bf16[512,2048]{1,0:T(8,128)(2,1)S(1)}) custom-call(s32[64,17]{1,0:T(8,128)S(1)} %bitcast.24), custom_call_target="tpu_custom_call" | custom-call | tf_op jit(solution)/shard_map/coverage/pallas_call | solution.py:228
  27.2 1.8 %fusion.5.padded = bf16[288,2176]{1,0:T(8,128)(2,1)S(1)} fusion(bf16[16,2048]{1,0:T(8,128)(2,1)S(1)} %collective-permute-done.1, bf16[256,2048]{1,0:T(8,128)(2,1)} %bitcast.26, bf16[16,2048]{1,0:T(8,128)(2,1)S(1)} %collective-permute-done), kind=kLoop, calls=%fused_computation.7 | loop fusion | flops 7520256 | bytes 2433024 | tf_op jit(solution)/shard_map/concatenate | solution.py:534
  29.0 2.9 %column_pass.1.source.images = bf16[7,288,2048]{2,1,0:T(8,128)(2,1)S(1)} custom-call(bf16[288,2176]{1,0:T(8,128)(2,1)S(1)} %fusion.5.padded, bf16[256,896]{1,0:T(8,128)(2,1)S(1)} %copy-done.2), custom_call_target="tpu_custom_call" | custom-call | tf_op jit(solution)/shard_map/column_pass/pallas_call | solution.py:253
  31.9 31.3 %normal_matrix.1 = f32[2,29,29]{2,1,0:T(8,128)S(1)} custom-call(bf16[7,288,2048]{2,1,0:T(8,128)(2,1)S(1)} %column_pass.1.source.images, bf16[1792,96]{1,0:T(8,128)(2,1)S(1)} %copy-done.3, bf16[512,2048]{1,0:T(8,128)(2,1)S(1)} %get-tuple-element.15.count), custom_call_target="tpu_custom_call" | custom-call | tf_op jit(solution)/shard_map/normal_matrix/pallas_call | solution.py:338
  63.3 3.2 %copy-done = bf16[7,288,2048]{2,1,0:T(8,128)(2,1)} copy-done((bf16[7,288,2048]{2,1,0:T(8,128)(2,1)}, bf16[7,288,2048]{2,1,0:T(8,128)(2,1)S(1)}, u32[]{:S(2)}) %copy-start) | copy-done | bytes 8257560
  66.6 30.3 %psum.7 = f32[2,29,29]{1,2,0:T(8,128)S(1)} all-reduce(f32[2,29,29]{1,2,0:T(8,128)S(1)} %copy.16), channel_id=1, replica_groups=mesh['patch'=8,'visit'=4] {'visit'}, use_global_device_ids=true, to_apply=%region_0.1 | all-reduce | flops 1682 | bytes 13456 | tf_op jit(solution)/shard_map/psum | solution.py:539
  96.9 0.1 copy.17
  97.0 5.3 %custom-call.8 = f32[2,29,29]{2,1,0:T(8,128)S(1)} custom-call(f32[2,29,29]{2,1,0:T(8,128)S(1)} %fusion.8), custom_call_target="Cholesky" | custom-call | tf_op jit(solution)/shard_map/jit(cholesky)/cholesky | solution.py:503
  102.3 0.1 compare_reduce_fusion
  102.5 4.5 %custom-call.9 = f32[2,1,29,29]{2,3,1,0:T(8,128)S(1)} custom-call(f32[2,1,29,29]{3,2,1,0:T(8,128)S(1)} %select_bitcast_fusion), custom_call_target="InvertDiagBlocksLowerTriangular" | custom-call | tf_op jit(solution)/shard_map/jit(_solve_triangular)/vmap()/triangular_solve | solution.py:504
  107.0 0.3 fusion.6
  107.2 0.2 fusion.12
  107.4 7.5 %all-to-all-done.1.got = bf16[64,16,2048]{2,1,0:T(8,128)(2,1)} async-done(((bf16[64,16,2048]{2,1,0:T(8,128)(2,1)}), bf16[64,16,2048]{2,1,0:T(8,128)(2,1)}, u32[]{:S(2)}, u32[]{:S(2)}) %all-to-all-start.1) | async-done | bytes 4194336 | tf_op jit(solution)/shard_map/all_to_all | solution.py:531
  115.0 13.0 %place_and_correlate.1 = (bf16[2,256,2048]{2,1,0:T(8,128)(2,1)S(1)}, f32[32,128]{1,0:T(8,128)S(1)}, bf16[7,288,2048]{2,1,0:T(8,128)(2,1)S(1)}) custom-call(bf16[64,16,2048]{2,1,0:T(8,128)(2,1)} %all-to-all-done.1.got, bf16[512,1024]{1,0:T(8,128)(2,1)S(1)} %get-tuple-element.14.placing, bf16[512,2048]{1,0:T(8,128)(2,1)S(1)} %get-tuple-element.15.count, ...), custom_call_target="tpu_custom_call" | custom-call | tf_op jit(solution)/shard_map/place_and_correlate/pallas_call | solution.py:414
  127.9 5.2 %all_gather.3.sums = f32[128,128]{1,0:T(8,128)S(1)} all-gather(f32[32,128]{1,0:T(8,128)S(1)} %get-tuple-element.17), channel_id=1, replica_groups=mesh['patch'=8,'visit'=4] {'visit'}, dimensions={0}, use_global_device_ids=true | all-gather | bytes 81920 | tf_op jit(solution)/shard_map/all_gather | solution.py:543
  133.2 3.8 %model_and_difference.1 = (bf16[2,256,2048]{2,1,0:T(8,128)(2,1)}, f32[2,29]{1,0:T(2,128)}) custom-call(f32[128,128]{1,0:T(8,128)S(1)} %all_gather.3.sums, f32[2,32,128]{2,1,0:T(8,128)S(1)} %pad.9.inverse, f32[7,64,96]{2,1,0:T(8,128)S(1)} %copy-done.1, bf16[7,288,2048]{2,1,0:T(8,128)(2,1)S(1)} %get-tuple-element.18.images, ...), custom_call_target="tpu_custom_call" | custom-call | tf_op jit(solution)/shard_map/model_and_difference/pallas_call | solution.py:482
  (17 shorter events, 0.3 us)
Async XLA Ops:
  2.2 14.6 %all-to-all-start = ((s32[32,2,17]{2,1,0:T(2,128)}), s32[32,2,17]{2,1,0:T(2,128)S(1)}, u32[]{:S(2)}, u32[]{:S(2)}) async-start(s32[32,2,17]{2,1,0:T(2,128)} %bitcast.27), calls=%async_computation | async-start | bytes 65536 | tf_op jit(solution)/shard_map/all_to_all | solution.py:528
  16.8 98.2 %all-to-all-start.1 = ((bf16[64,16,2048]{2,1,0:T(8,128)(2,1)}), bf16[64,16,2048]{2,1,0:T(8,128)(2,1)}, u32[]{:S(2)}, u32[]{:S(2)}) async-start(bf16[64,16,2048]{2,1,0:T(8,128)(2,1)} %pack_blocks.1), calls=%async_computation.1 | async-start | bytes 8388608 | tf_op jit(solution)/shard_map/all_to_all | solution.py:531
  20.4 8.5 %copy-start.2 = (bf16[256,896]{1,0:T(8,128)(2,1)S(1)}, bf16[256,896]{1,0:T(8,128)(2,1)}, u32[]{:S(2)}) copy-start(bf16[256,896]{1,0:T(8,128)(2,1)} %constant.55.clone.table) | copy-start | bytes 1376260
  21.4 5.8 %collective-permute-start.1 = (bf16[16,2048]{1,0:T(8,128)(2,1)S(1)}, bf16[16,2048]{1,0:T(8,128)(2,1)S(1)}, u32[]{:S(2)}, u32[]{:S(2)}) collective-permute-start(bf16[16,2048]{1,0:T(8,128)(2,1)S(1)} %get-tuple-element.27), channel_id=1, source_target_pairs={{1,0},{2,1},{3,2},{5,4},{6,5},{7,6},{9,8},{10,9},{11,10},{13,12},{... | collective-permute-start | bytes 196616 | tf_op jit(solution)/shard_map/ppermute | solution.py:513
  22.7 4.5 %collective-permute-start = (bf16[16,2048]{1,0:T(8,128)(2,1)S(1)}, bf16[16,2048]{1,0:T(8,128)(2,1)S(1)}, u32[]{:S(2)}, u32[]{:S(2)}) collective-permute-start(bf16[16,2048]{1,0:T(8,128)(2,1)S(1)} %get-tuple-element.26), channel_id=1, source_target_pairs={{0,1},{1,2},{2,3},{4,5},{5,6},{6,7},{8,9},{9,10},{10,11},{12,13},{... | collective-permute-start | bytes 196616 | tf_op jit(solution)/shard_map/ppermute | solution.py:512
  29.0 2.9 %copy-start.3 = (bf16[1792,96]{1,0:T(8,128)(2,1)S(1)}, bf16[1792,96]{1,0:T(8,128)(2,1)}, u32[]{:S(2)}) copy-start(bf16[1792,96]{1,0:T(8,128)(2,1)} %constant.56.clone.table) | copy-start | bytes 1032196
  31.9 83.1 %copy-start.1 = (f32[7,64,96]{2,1,0:T(8,128)S(1)}, f32[7,64,96]{2,1,0:T(8,128)}, u32[]{:S(2)}) copy-start(f32[7,64,96]{2,1,0:T(8,128)} %constant.57.clone.table) | copy-start | bytes 516100
  63.3 3.2 %copy-start = (bf16[7,288,2048]{2,1,0:T(8,128)(2,1)}, bf16[7,288,2048]{2,1,0:T(8,128)(2,1)S(1)}, u32[]{:S(2)}) copy-start(bf16[7,288,2048]{2,1,0:T(8,128)(2,1)S(1)} %column_pass.1.source.images) | copy-start | bytes 24772612

commit v2 on v1

--- a/solution.py
+++ b/solution.py
@@ -191,7 +191,7 @@
     )(*(pltpu.with_memory_space_constraint(item, pltpu.HBM) for item in (dest, flags, blocks)))
 
 
-def cover_kernel(meta, placing, spread):
+def cover_kernel(meta, placing, spread, factor):
     slots = meta.shape[0]
     cols = spread.shape[1]
     lines = placing.shape[1]
@@ -215,6 +215,7 @@
         row = lax.broadcasted_iota(jnp.int32, (step, lines), 0) + k * step
         placing[k * step : (k + 1) * step, :] = jnp.where(row == target, 1.0, 0.0).astype(jnp.bfloat16)
     counted = lax.dot_general(placing[...], good, (((1,), (1,)), ((), ())), preferred_element_type=jnp.float32)
+    factor[...] = jnp.minimum(counted, 1.0) / jnp.maximum(counted, 1.0)
     wide_group = cols // GROUPS
     for q in range(GROUPS):
         spread[:, q * wide_group : (q + 1) * wide_group] = jnp.broadcast_to(
@@ -230,9 +231,10 @@
         out_shape=(
             jax.ShapeDtypeStruct((VISITS * row_count, slots * BLOCK_ROWS), jnp.bfloat16),
             jax.ShapeDtypeStruct((VISITS * row_count, cols), jnp.bfloat16),
+            jax.ShapeDtypeStruct((VISITS * row_count, 128), jnp.float32),
         ),
         in_specs=[vmem],
-        out_specs=(vmem, vmem),
+        out_specs=(vmem, vmem, vmem),
         compiler_params=params(24),
         name="coverage",
     )(got_meta)
@@ -349,10 +351,17 @@
     )(images, table, count)
 
 
-def place_kernel(got, placing, count, source, table, science, sums, images, buf, acc, sem_got, sem_img):
+ONES_ROWS = 16
+PLACE_CHUNK = 512
+
+
+def place_kernel(got, placing, factor_hbm, source, table, science, sums, images, buf, acc, factor, sem_got, sem_img, sem_small):
     rows = science.shape[1]
     cols = science.shape[2]
-    chunk = 256
+    chunk = PLACE_CHUNK
+    group = cols // GROUPS
+    small = pltpu.make_async_copy(factor_hbm, factor, sem_small)
+    small.start()
     copies = []
     for c in range(cols // chunk):
         lanes = slice(c * chunk, (c + 1) * chunk)
@@ -362,29 +371,37 @@
                 pltpu.make_async_copy(source.at[:, :, lanes], images.at[:, :, lanes], sem_img.at[c]),
             )
         )
-        for item in copies[-1]:
-            item.start()
+    for item in copies[0]:
+        item.start()
     partial = None
-    total = [jnp.zeros((8, 128), jnp.float32) for _ in range(VISITS)]
+    ones = jnp.ones((ONES_ROWS, chunk), jnp.bfloat16)
     for c in range(cols // chunk):
         lanes = slice(c * chunk, (c + 1) * chunk)
         copies[c][0].wait()
+        if c + 1 < len(copies):
+            copies[c + 1][0].start()
         summed = jnp.dot(placing[...], buf[:, :, lanes].reshape(-1, chunk), preferred_element_type=jnp.float32)
-        spread = count[:, lanes].astype(jnp.float32)
-        value = (summed / jnp.maximum(spread, 1.0)).astype(jnp.bfloat16)
-        weighted = value * jnp.minimum(spread, 1.0).astype(jnp.bfloat16)
+        if c == 0:
+            small.wait()
+        spread = jnp.concatenate(
+            [
+                jnp.broadcast_to(factor[:, q : q + 1], (VISITS * rows, group))
+                for q in range(c * chunk // group, (c + 1) * chunk // group)
+            ],
+            axis=1,
+        )
+        value = (summed * spread).astype(jnp.bfloat16)
         for v in range(VISITS):
             science[v, :, lanes] = value[v * rows : (v + 1) * rows, :]
-            part = weighted[v * rows : (v + 1) * rows, :].astype(jnp.float32)
-            fold = jnp.sum(part.reshape(rows // 8, 8, chunk), axis=0)
-            for k in range(chunk // 128):
-                total[v] = total[v] + fold[:, k * 128 : (k + 1) * 128]
         copies[c][1].wait()
+        if c + 1 < len(copies):
+            copies[c + 1][1].start()
         for t in range(rows // TILE):
             left = jnp.concatenate(
-                [weighted[v * rows + t * TILE : v * rows + (t + 1) * TILE, :] for v in range(VISITS)], axis=0
+                [value[v * rows + t * TILE : v * rows + (t + 1) * TILE, :] for v in range(VISITS)], axis=0
             )
             right = images[:, t * TILE : t * TILE + SPAN, lanes].reshape(NPOW * SPAN, chunk)
+            right = jnp.concatenate([right, ones], axis=0)
             product = lax.dot_general(left, right, (((1,), (1,)), ((), ())), preferred_element_type=jnp.float32)
             partial = product if partial is None else partial + product
     acc[...] = partial
@@ -399,15 +416,14 @@
                 parts.append(jnp.sum(cross * table[i], axis=0, keepdims=True))
         parts.append(jnp.zeros((32 - BASIS_COUNT, SPAN), jnp.float32))
         item = jnp.sum(jnp.concatenate(parts, axis=0), axis=1, keepdims=True)
-        flat = jnp.sum(jnp.sum(total[v], axis=0, keepdims=True), axis=1, keepdims=True)
+        flat = jnp.sum(acc[v * TILE : (v + 1) * TILE, NPOW * SPAN : NPOW * SPAN + 1], axis=0, keepdims=True)
         item = jnp.where(row_id == BASIS_COUNT, flat, item)
         result = result + jnp.where(lane_id == v, item, 0.0)
     sums[...] = result
 
 
-def place(got, placing, count, images, bands, row_count):
+def place(got, placing, factor, images, bands, row_count):
     slots, _, cols = got.shape
-    chunks = cols // 256
     table = jnp.asarray(bands)
     vmem = pl.BlockSpec(memory_space=pltpu.VMEM)
     hbm = pl.BlockSpec(memory_space=pltpu.HBM)
@@ -418,20 +434,22 @@
             jax.ShapeDtypeStruct((32, 128), jnp.float32),
             jax.ShapeDtypeStruct(images.shape, jnp.bfloat16),
         ),
-        in_specs=[hbm, vmem, vmem, hbm, vmem],
+        in_specs=[hbm, vmem, hbm, hbm, vmem],
         out_specs=(vmem, vmem, vmem),
         scratch_shapes=[
             pltpu.VMEM(got.shape, jnp.bfloat16),
-            pltpu.VMEM((VISITS * TILE, NPOW * SPAN), jnp.float32),
-            pltpu.SemaphoreType.DMA((chunks,)),
-            pltpu.SemaphoreType.DMA((chunks,)),
+            pltpu.VMEM((VISITS * TILE, NPOW * SPAN + ONES_ROWS), jnp.float32),
+            pltpu.VMEM(factor.shape, jnp.float32),
+            pltpu.SemaphoreType.DMA((cols // PLACE_CHUNK,)),
+            pltpu.SemaphoreType.DMA((cols // PLACE_CHUNK,)),
+            pltpu.SemaphoreType.DMA,
         ],
         compiler_params=params(40),
         name="place_and_correlate",
     )(
         pltpu.with_memory_space_constraint(got, pltpu.HBM),
         placing,
-        count,
+        pltpu.with_memory_space_constraint(factor, pltpu.HBM),
         pltpu.with_memory_space_constraint(images, pltpu.HBM),
         table,
     )
@@ -468,7 +486,7 @@
                 full = model[v * TILE : (v + 1) * TILE, :] + level[v]
                 seen = count[v * rows + t * TILE : v * rows + (t + 1) * TILE, lanes]
                 weight = jnp.minimum(seen.astype(jnp.float32), 1.0)
-                buf[v, at, lanes] = (weight * (science[v, at, lanes].astype(jnp.float32) - full)).astype(jnp.bfloat16)
+                buf[v, at, lanes] = (science[v, at, lanes].astype(jnp.float32) - weight * full).astype(jnp.bfloat16)
         copies.append(pltpu.make_async_copy(buf.at[:, :, lanes], out.at[:, :, lanes], sem.at[c]))
         copies[-1].start()
     for item in copies:
@@ -534,12 +552,13 @@
     tall = jnp.concatenate([above, rows, below], axis=0)
     padded = jnp.pad(tall, ((0, 0), (HALF_TAPS, 128 - HALF_TAPS)))
     images = column_pass(padded, taps, cols)
-    placing, count = cover(got_meta, row_count, cols)
-
-    normal = lax.psum(gram(images, count, taps), "visit")
+    placing, count, factor = cover(got_meta, row_count, cols)
+
+    shares = lax.all_gather(gram(images, count, taps), "visit", axis=0, tiled=False)
+    normal = jnp.sum(shares, axis=0)
     inverse = jnp.pad(inverse_of(normal), ((0, 0), (0, 32 - TERMS), (0, 128 - TERMS)))
 
-    science, sums, images = place(got, placing, count, images, bands, row_count)
+    science, sums, images = place(got, placing, factor, images, bands, row_count)
     sums = lax.all_gather(sums, "visit", axis=0, tiled=True)
     difference, coeffs = model(sums, inverse, images, science, count, bands)
     return (difference[:, None], coeffs[:, None])

time: 138 us -> 134 us (0.971)
  waiting for transfers between devices: 11 us -> 18.8 us
  blocking collectives: 35.5 us -> 27.8 us
  Pallas kernels: 57.8 us -> 54.5 us
  local copies, waits for them, and re-layouts: 4.35 us -> 1.71 us
  other arithmetic: 11.8 us -> 14.3 us
    psum x1 -> x0, blocking collectives: 30.3 us -> none  [body(): normal = lax.psum(gram(images, count, taps), 'visit')]
    all_gather x0 -> x1, blocking collectives: none -> 22.5 us  [body(): lax.all_gather(gram(images, count, taps), 'visit', axis=0, tiled=False)]
    all_to_all x1, waiting for transfers between devices: 7.55 us -> 15.4 us  [body(): got = lax.all_to_all(send, axes, split_axis=0, concat_axis=0, tiled=True)]
    pallas_call x1, Pallas kernels: 13 us -> 9.69 us  [place(): pl.pallas_call(place_kernel, out_shape=(jax.ShapeDtypeStruct((VISITS, row...]
    unnamed x8 -> x10, local copies, waits for them, and re-layouts: 3.2 us -> 0.73 us
  transfers between devices with their start and end apart: 4 -> 4, of which waited for: 2 -> 2; matrix products, arithmetic and copies ran while one was open for 10% -> 12% of each run, Pallas kernels for 29% -> 29%
where the time goes in v2:
time: 134 us
  Pallas kernels  54.5 us (41%)
  blocking collectives  27.8 us (21%)
  waiting for transfers between devices  18.8 us (14%)
  starting transfers between devices  15.2 us (11%)
  other arithmetic  14.3 us (11%)
  local copies, waits for them, and re-layouts  1.71 us (1%)
    pallas_call x1, Pallas kernels, gram(): pl.pallas_call(gram_kernel, out_shape=jax.ShapeDtypeStruct((VISITS, TERMS...  31.3 us
    all_gather x1, blocking collectives, body(): lax.all_gather(gram(images, count, taps), 'visit', axis=0, tiled=False)  22.5 us
    all_to_all x1, waiting for transfers between devices, body(): got = lax.all_to_all(send, axes, split_axis=0, concat_axis=0, tiled=True)  15.4 us
    pallas_call x1, Pallas kernels, place(): pl.pallas_call(place_kernel, out_shape=(jax.ShapeDtypeStruct((VISITS, row...  9.69 us
    all_to_all x1, starting transfers between devices, body(): lax.all_to_all(meta, axes, split_axis=0, concat_axis=0, tiled=True)  7.3 us
    another operation x4, other arithmetic, inverse_of(): lower = jnp.linalg.cholesky(matrix)  6.74 us
    another operation x3, other arithmetic, inverse_of(): half = jax.scipy.linalg.solve_triangular(lower, eye, lower=True)  5.79 us
    all_gather x1, blocking collectives, body(): sums = lax.all_gather(sums, 'visit', axis=0, tiled=True)  5.25 us
  transfers between devices with their start and end apart: 4, of which 2 were waited for; matrix products, arithmetic and copies ran while one was open for 12% of the time, Pallas kernels for 29%

profile of v2, /device:TPU:0, one launch (start us, length us, event | category | flops | bytes accessed | tf_op | source)
XLA Modules:
  0.0 133.9 jit_solution(4185827671110983178)
XLA Ops:
  0.6 1.6 %describe_blocks.1 = s32[64,17]{1,0:T(8,128)} custom-call(s32[1,32]{1,0:T(1,128)} %bitcast.32, s32[1,32]{1,0:T(1,128)} %bitcast.33, s32[1,32]{1,0:T(1,128)} %bitcast.34, s32[16,32]{1,0:T(8,128)} %bitcast.30), custom_call_target="tpu_custom_call" | custom-call | tf_op jit(solution)/shard_map/describe_blocks/pallas_call | solution.py:96
  2.2 7.3 %all-to-all-start = ((s32[32,2,17]{2,1,0:T(2,128)}), s32[32,2,17]{2,1,0:T(2,128)S(1)}, u32[]{:S(2)}, u32[]{:S(2)}) async-start(s32[32,2,17]{2,1,0:T(2,128)} %bitcast.29), calls=%async_computation | async-start | bytes 65536 | tf_op jit(solution)/shard_map/all_to_all | solution.py:546
  9.5 3.8 %pack_blocks.1 = bf16[64,16,2048]{2,1,0:T(8,128)(2,1)} custom-call(s32[32]{0:T(128)} %dest_hbm.1, s32[16,32]{1,0:T(8,128)} %bitcast.31, bf16[32,16,2048]{2,1,0:T(8,128)(2,1)} %blocks.1), custom_call_target="tpu_custom_call" | custom-call | tf_op jit(solution)/shard_map/pack_blocks/pallas_call | solution.py:171
  13.3 3.5 %all-to-all-done = s32[32,2,17]{2,1,0:T(2,128)S(1)} async-done(((s32[32,2,17]{2,1,0:T(2,128)}), s32[32,2,17]{2,1,0:T(2,128)S(1)}, u32[]{:S(2)}, u32[]{:S(2)}) %all-to-all-start) | async-done | bytes 4384 | tf_op jit(solution)/shard_map/all_to_all | solution.py:546
  16.8 3.6 %all-to-all-start.1 = ((bf16[64,16,2048]{2,1,0:T(8,128)(2,1)}), bf16[64,16,2048]{2,1,0:T(8,128)(2,1)}, u32[]{:S(2)}, u32[]{:S(2)}) async-start(bf16[64,16,2048]{2,1,0:T(8,128)(2,1)} %pack_blocks.1), calls=%async_computation.1 | async-start | bytes 8388608 | tf_op jit(solution)/shard_map/all_to_all | solution.py:549
  20.4 0.6 iota_compare_fusion.2
  21.0 0.9 fusion.11
  21.9 1.3 collective-permute-start.1
  23.2 3.0 %collective-permute-start = (bf16[16,2048]{1,0:T(8,128)(2,1)S(1)}, bf16[16,2048]{1,0:T(8,128)(2,1)S(1)}, u32[]{:S(2)}, u32[]{:S(2)}) collective-permute-start(bf16[16,2048]{1,0:T(8,128)(2,1)S(1)} %get-tuple-element.30), channel_id=1, source_target_pairs={{0,1},{1,2},{2,3},{4,5},{5,6},{6,7},{8,9},{9,10},{10,11},{12,13},{... | collective-permute-start | bytes 196616 | tf_op jit(solution)/shard_map/ppermute | solution.py:530
  26.2 0.6 iota_compare_fusion.3
  26.8 1.4 %coverage.1 = (bf16[512,1024]{1,0:T(8,128)(2,1)S(1)}, bf16[512,2048]{1,0:T(8,128)(2,1)S(1)}, f32[512,128]{1,0:T(8,128)S(1)}) custom-call(s32[64,17]{1,0:T(8,128)S(1)} %bitcast.25), custom_call_target="tpu_custom_call" | custom-call | tf_op jit(solution)/shard_map/coverage/pallas_call | solution.py:229
  28.3 0.7 copy-done.4
  29.0 1.8 %fusion.5.padded = bf16[288,2176]{1,0:T(8,128)(2,1)S(1)} fusion(bf16[16,2048]{1,0:T(8,128)(2,1)S(1)} %collective-permute-done.1, bf16[256,2048]{1,0:T(8,128)(2,1)} %bitcast.27, bf16[16,2048]{1,0:T(8,128)(2,1)S(1)} %collective-permute-done), kind=kLoop, calls=%fused_computation.7 | loop fusion | flops 7520256 | bytes 2433024 | tf_op jit(solution)/shard_map/concatenate | solution.py:552
  30.8 2.9 %column_pass.1.source.images = bf16[7,288,2048]{2,1,0:T(8,128)(2,1)S(1)} custom-call(bf16[288,2176]{1,0:T(8,128)(2,1)S(1)} %fusion.5.padded, bf16[256,896]{1,0:T(8,128)(2,1)S(1)} %copy-done.2), custom_call_target="tpu_custom_call" | custom-call | tf_op jit(solution)/shard_map/column_pass/pallas_call | solution.py:255
  33.7 31.3 %normal_matrix.1 = f32[2,29,29]{2,1,0:T(8,128)S(1)} custom-call(bf16[7,288,2048]{2,1,0:T(8,128)(2,1)S(1)} %column_pass.1.source.images, bf16[1792,96]{1,0:T(8,128)(2,1)S(1)} %copy-done.3, bf16[512,2048]{1,0:T(8,128)(2,1)S(1)} %get-tuple-element.19.count), custom_call_target="tpu_custom_call" | custom-call | tf_op jit(solution)/shard_map/normal_matrix/pallas_call | solution.py:340
  65.1 22.5 %all-gather = f32[8,29,29]{2,1,0:T(8,128)S(1)} all-gather(f32[2,29,29]{2,1,0:T(8,128)S(1)} %normal_matrix.1), channel_id=2, replica_groups=mesh['patch'=8,'visit'=4] {'visit'}, dimensions={0}, use_global_device_ids=true | all-gather | bytes 33640 | tf_op jit(solution)/shard_map/all_gather | solution.py:557
  87.7 5.3 %custom-call.8 = f32[2,29,29]{2,1,0:T(8,128)S(1)} custom-call(f32[2,29,29]{2,1,0:T(8,128)S(1)} %fusion.8), custom_call_target="Cholesky" | custom-call | tf_op jit(solution)/shard_map/jit(cholesky)/cholesky | solution.py:521
  93.1 0.7 select_reduce_fusion
  93.9 0.7 select_bitcast_fusion
  94.6 4.4 %custom-call.9 = f32[2,1,29,29]{2,3,1,0:T(8,128)S(1)} custom-call(f32[2,1,29,29]{3,2,1,0:T(8,128)S(1)} %select_bitcast_fusion), custom_call_target="InvertDiagBlocksLowerTriangular" | custom-call | tf_op jit(solution)/shard_map/jit(_solve_triangular)/vmap()/triangular_solve | solution.py:522
  99.6 15.4 %all-to-all-done.1.got = bf16[64,16,2048]{2,1,0:T(8,128)(2,1)} async-done(((bf16[64,16,2048]{2,1,0:T(8,128)(2,1)}), bf16[64,16,2048]{2,1,0:T(8,128)(2,1)}, u32[]{:S(2)}, u32[]{:S(2)}) %all-to-all-start.1) | async-done | bytes 4194336 | tf_op jit(solution)/shard_map/all_to_all | solution.py:549
  115.0 9.7 %place_and_correlate.1 = (bf16[2,256,2048]{2,1,0:T(8,128)(2,1)S(1)}, f32[32,128]{1,0:T(8,128)S(1)}, bf16[7,288,2048]{2,1,0:T(8,128)(2,1)S(1)}) custom-call(bf16[64,16,2048]{2,1,0:T(8,128)(2,1)} %all-to-all-done.1.got, bf16[512,1024]{1,0:T(8,128)(2,1)S(1)} %get-tuple-element.15.placing, f32[512,128]{1,0:T(8,128)} %copy-done.4, bf16[7,288,2048]{2,1,0:T(8,128)(2,1)} %copy-done, ...), custom_call_target="tpu_custom_call" | custom-call | tf_op jit(solution)/shard_map/place_and_correlate/pallas_call | solution.py:430
  124.7 5.2 %all_gather.9.sums = f32[128,128]{1,0:T(8,128)S(1)} all-gather(f32[32,128]{1,0:T(8,128)S(1)} %get-tuple-element.18), channel_id=1, replica_groups=mesh['patch'=8,'visit'=4] {'visit'}, dimensions={0}, use_global_device_ids=true | all-gather | bytes 81920 | tf_op jit(solution)/shard_map/all_gather | solution.py:562
  129.9 3.8 %model_and_difference.1 = (bf16[2,256,2048]{2,1,0:T(8,128)(2,1)}, f32[2,29]{1,0:T(2,128)}) custom-call(f32[128,128]{1,0:T(8,128)S(1)} %all_gather.9.sums, f32[2,32,128]{2,1,0:T(8,128)S(1)} %pad.9.inverse, f32[7,64,96]{2,1,0:T(8,128)S(1)} %copy-done.1, bf16[7,288,2048]{2,1,0:T(8,128)(2,1)S(1)} %get-tuple-element.20.images, ...), custom_call_target="tpu_custom_call" | custom-call | tf_op jit(solution)/shard_map/model_and_difference/pallas_call | solution.py:500
  (19 shorter events, 0.8 us)
Async XLA Ops:
  2.2 14.6 %all-to-all-start = ((s32[32,2,17]{2,1,0:T(2,128)}), s32[32,2,17]{2,1,0:T(2,128)S(1)}, u32[]{:S(2)}, u32[]{:S(2)}) async-start(s32[32,2,17]{2,1,0:T(2,128)} %bitcast.29), calls=%async_computation | async-start | bytes 65536 | tf_op jit(solution)/shard_map/all_to_all | solution.py:546
  16.8 98.2 %all-to-all-start.1 = ((bf16[64,16,2048]{2,1,0:T(8,128)(2,1)}), bf16[64,16,2048]{2,1,0:T(8,128)(2,1)}, u32[]{:S(2)}, u32[]{:S(2)}) async-start(bf16[64,16,2048]{2,1,0:T(8,128)(2,1)} %pack_blocks.1), calls=%async_computation.1 | async-start | bytes 8388608 | tf_op jit(solution)/shard_map/all_to_all | solution.py:549
  20.4 10.3 %copy-start.2 = (bf16[256,896]{1,0:T(8,128)(2,1)S(1)}, bf16[256,896]{1,0:T(8,128)(2,1)}, u32[]{:S(2)}) copy-start(bf16[256,896]{1,0:T(8,128)(2,1)} %constant.56.clone.table) | copy-start | bytes 1376260
  21.9 7.1 %collective-permute-start.1 = (bf16[16,2048]{1,0:T(8,128)(2,1)S(1)}, bf16[16,2048]{1,0:T(8,128)(2,1)S(1)}, u32[]{:S(2)}, u32[]{:S(2)}) collective-permute-start(bf16[16,2048]{1,0:T(8,128)(2,1)S(1)} %get-tuple-element.31), channel_id=1, source_target_pairs={{1,0},{2,1},{3,2},{5,4},{6,5},{7,6},{9,8},{10,9},{11,10},{13,12},{... | collective-permute-start | bytes 196616 | tf_op jit(solution)/shard_map/ppermute | solution.py:531
  23.2 5.8 %collective-permute-start = (bf16[16,2048]{1,0:T(8,128)(2,1)S(1)}, bf16[16,2048]{1,0:T(8,128)(2,1)S(1)}, u32[]{:S(2)}, u32[]{:S(2)}) collective-permute-start(bf16[16,2048]{1,0:T(8,128)(2,1)S(1)} %get-tuple-element.30), channel_id=1, source_target_pairs={{0,1},{1,2},{2,3},{4,5},{5,6},{6,7},{8,9},{9,10},{10,11},{12,13},{... | collective-permute-start | bytes 196616 | tf_op jit(solution)/shard_map/ppermute | solution.py:530
  28.3 0.7 copy-start.4
  30.8 3.0 %copy-start.3 = (bf16[1792,96]{1,0:T(8,128)(2,1)S(1)}, bf16[1792,96]{1,0:T(8,128)(2,1)}, u32[]{:S(2)}) copy-start(bf16[1792,96]{1,0:T(8,128)(2,1)} %constant.57.clone.table) | copy-start | bytes 1032196
  33.7 31.4 %copy-start = (bf16[7,288,2048]{2,1,0:T(8,128)(2,1)}, bf16[7,288,2048]{2,1,0:T(8,128)(2,1)S(1)}, u32[]{:S(2)}) copy-start(bf16[7,288,2048]{2,1,0:T(8,128)(2,1)S(1)} %column_pass.1.source.images) | copy-start | bytes 24772612
  33.7 81.3 %copy-start.1 = (f32[7,64,96]{2,1,0:T(8,128)S(1)}, f32[7,64,96]{2,1,0:T(8,128)}, u32[]{:S(2)}) copy-start(f32[7,64,96]{2,1,0:T(8,128)} %constant.58.clone.table) | copy-start | bytes 516100

commit v3 on v2

--- a/solution.py
+++ b/solution.py
@@ -65,46 +65,150 @@
     return pltpu.CompilerParams(vmem_limit_bytes=mib * MIB)
 
 
-def describe_kernel(dest, offset, visit, bad, meta, row_count):
-    count = dest.shape[1]
-    slots = meta.shape[0]
-    goal = jnp.broadcast_to(dest[...].astype(jnp.float32), (count, count))
+FIRST = 4
+META_ROWS = 8
+
+
+def first_kernel(dest_row_hbm, offset_hbm, visit_hbm, flags_hbm, dest_hbm, blocks, send, dest_row, offset, visit, flags, dest, buf, out, zero, wide, narrow, cnt, where, sem_small, sem_in, sem_out, row_count):
+    count = blocks.shape[0]
+    sources = send.shape[0]
+    data_rows = SLOT_CAP * FIRST * BLOCK_ROWS
+    slot_rows = FIRST * BLOCK_ROWS
+    width = buf.shape[2]
+    small = [
+        pltpu.make_async_copy(source, target, sem_small.at[k])
+        for k, (source, target) in enumerate(
+            (
+                (dest_hbm, dest),
+                (dest_row_hbm, dest_row),
+                (offset_hbm, offset),
+                (visit_hbm, visit),
+                (flags_hbm, flags),
+            )
+        )
+    ]
+    for item in small:
+        item.start()
+    group = min(8, count)
+    loads = []
+    for k in range(count // group):
+        part = pl.ds(k * group, group)
+        loads.append(pltpu.make_async_copy(blocks.at[part, :, pl.ds(0, width)], buf.at[part], sem_in.at[k]))
+        loads[-1].start()
+    zero[...] = jnp.zeros_like(zero)
+
+    def reset(d, carry):
+        cnt[d] = 0
+        return carry
+
+    def locate(n, carry):
+        d = dest[n]
+        rank = cnt[d]
+        cnt[d] = rank + 1
+        where[n] = rank
+        return carry
+
+    def blank(d, carry):
+        for r in range(SLOT_CAP):
+
+            @pl.when(cnt[d] <= r)
+            def _():
+                pltpu.make_async_copy(zero, send.at[d, pl.ds(r * slot_rows, slot_rows)], sem_out).start()
+
+        return carry
+
+    lax.fori_loop(0, sources, reset, 0, unroll=8)
+    for item in small:
+        item.wait()
+    lax.fori_loop(0, count, locate, 0, unroll=4)
+    lax.fori_loop(0, sources, blank, 0, unroll=4)
+    goal = jnp.broadcast_to(dest_row[...].astype(jnp.float32), (count, count))
     earlier = lax.broadcasted_iota(jnp.int32, (count, count), 0) < lax.broadcasted_iota(jnp.int32, (count, count), 1)
     rank = jnp.sum(jnp.where((jnp.transpose(goal) == goal) & earlier, 1.0, 0.0), axis=0, keepdims=True)
-    slot = goal[0:1, :] * SLOT_CAP + rank
-    own = lax.broadcasted_iota(jnp.int32, (slots, count), 0).astype(jnp.float32) == slot
-    pick = jnp.where(own, 1.0, 0.0)
-    start = (visit[...] * row_count + offset[...] + 1).astype(jnp.float32)
-    landing = jnp.sum(jnp.where(own, start, 0.0), axis=1, keepdims=True) - 1.0
-    words = lax.dot_general(
-        pick,
-        bad[...].astype(jnp.float32),
-        (((1,), (1,)), ((), ())),
-        precision=lax.Precision.HIGHEST,
-        preferred_element_type=jnp.float32,
+    line = goal[0:1, :] * META_ROWS + rank * 4
+    bits = flags[...]
+    start = visit[...] * row_count + offset[...] + 1
+    row16 = lax.broadcasted_iota(jnp.int32, (BLOCK_ROWS, count), 0)
+    start = jnp.broadcast_to(start, (BLOCK_ROWS, count))
+    kinds = (
+        jnp.bitwise_and(bits, 255),
+        jnp.right_shift(bits, 8),
+        jnp.where(row16 == 0, jnp.bitwise_and(start, 255), jnp.where(row16 == 1, jnp.right_shift(start, 8), 0)),
     )
-    meta[:, 0:BLOCK_ROWS] = words.astype(jnp.int32)
-    meta[:, BLOCK_ROWS : BLOCK_ROWS + 1] = landing.astype(jnp.int32)
-
-
-def describe(dest, offset, visit_id, flags, slots, row_count):
-    vmem = pl.BlockSpec(memory_space=pltpu.VMEM)
+    row_id = lax.broadcasted_iota(jnp.int32, (sources * META_ROWS, count), 0).astype(jnp.float32)
+    total = jnp.zeros((sources * META_ROWS, BLOCK_ROWS), jnp.float32)
+    for t, kind in enumerate(kinds):
+        pick = jnp.where(row_id == line + t, 1.0, 0.0).astype(jnp.bfloat16)
+        total = total + lax.dot_general(
+            pick,
+            kind.astype(jnp.float32).astype(jnp.bfloat16),
+            (((1,), (1,)), ((), ())),
+            preferred_element_type=jnp.float32,
+        )
+    wide[...] = jnp.zeros_like(wide)
+    wide[:, 0:BLOCK_ROWS] = total
+    narrow[...] = wide[...].reshape(sources, META_ROWS, 128).astype(jnp.bfloat16)
+    label = pltpu.make_async_copy(narrow, send.at[:, pl.ds(data_rows, META_ROWS), :], sem_small.at[len(small)])
+    label.start()
+    for k in range(count // group):
+        loads[k].wait()
+        for n in range(k * group, (k + 1) * group):
+            word = jnp.broadcast_to(flags[:, n : n + 1], (BLOCK_ROWS, 128))
+            for q in range(FIRST):
+                good = (1 - jnp.bitwise_and(jnp.right_shift(word, q), 1)).astype(jnp.float32).astype(jnp.bfloat16)
+                out[n, q * BLOCK_ROWS : (q + 1) * BLOCK_ROWS, :] = buf[n, :, q * 128 : (q + 1) * 128] * good
+            target = send.at[dest[n], pl.ds(pl.multiple_of(where[n] * slot_rows, slot_rows), slot_rows)]
+            pltpu.make_async_copy(out.at[n], target, sem_out).start()
+    whole = send.at[:, pl.ds(0, data_rows), :]
+    pltpu.make_async_copy(whole, whole, sem_out).wait()
+    label.wait()
+
+
+def pack_first(dest, offset, visit_id, flags, blocks, sources, row_count):
+    count, _, cols = blocks.shape
+    width = cols // GROUPS * FIRST
+    hbm = pl.BlockSpec(memory_space=pltpu.HBM)
+    slot_rows = FIRST * BLOCK_ROWS
 
     def kernel(*refs):
-        describe_kernel(*refs, row_count=row_count)
+        first_kernel(*refs, row_count=row_count)
 
     return pl.pallas_call(
         kernel,
-        out_shape=jax.ShapeDtypeStruct((slots, 1 + BLOCK_ROWS), jnp.int32),
-        in_specs=[vmem] * 4,
-        out_specs=vmem,
-        name="describe_blocks",
-    )(dest[None, :], offset[None, :], visit_id[None, :], flags)
+        out_shape=pltpu.HBM((sources, SLOT_CAP * slot_rows + META_ROWS, 128), jnp.bfloat16),
+        in_specs=[hbm] * 6,
+        out_specs=hbm,
+        scratch_shapes=[
+            pltpu.VMEM((1, count), jnp.int32),
+            pltpu.VMEM((1, count), jnp.int32),
+            pltpu.VMEM((1, count), jnp.int32),
+            pltpu.VMEM((BLOCK_ROWS, count), jnp.int32),
+            pltpu.SMEM((count,), jnp.int32),
+            pltpu.VMEM((count, BLOCK_ROWS, width), jnp.bfloat16),
+            pltpu.VMEM((count, slot_rows, 128), jnp.bfloat16),
+            pltpu.VMEM((slot_rows, 128), jnp.bfloat16),
+            pltpu.VMEM((sources * META_ROWS, 128), jnp.float32),
+            pltpu.VMEM((sources, META_ROWS, 128), jnp.bfloat16),
+            pltpu.SMEM((sources,), jnp.int32),
+            pltpu.SMEM((count,), jnp.int32),
+            pltpu.SemaphoreType.DMA((6,)),
+            pltpu.SemaphoreType.DMA((max(1, count // 8),)),
+            pltpu.SemaphoreType.DMA,
+        ],
+        compiler_params=params(24),
+        name="pack_first_groups",
+    )(
+        *(
+            pltpu.with_memory_space_constraint(item, pltpu.HBM)
+            for item in (dest[None, :], offset[None, :], visit_id[None, :], flags, dest, blocks)
+        )
+    )
 
 
 def pack_kernel(dest_hbm, bad_hbm, blocks, send, dest, bad, buf, out, zero, spread, cnt, where, sem_small, sem_in, sem_out):
     count = blocks.shape[0]
-    cols = blocks.shape[2]
+    cols = send.shape[2]
+    skip = blocks.shape[2] - cols
     slots = send.shape[0]
     group = min(8, count)
     small = [
@@ -115,7 +219,7 @@
         item.start()
     for k in range(count // group):
         part = pl.ds(k * group, group)
-        pltpu.make_async_copy(blocks.at[part], buf.at[part], sem_in.at[k]).start()
+        pltpu.make_async_copy(blocks.at[part, :, pl.ds(skip, cols)], buf.at[part], sem_in.at[k]).start()
 
     def reset(d, carry):
         cnt[d] = 0
@@ -145,7 +249,7 @@
     lax.fori_loop(0, slots // SLOT_CAP, blank, 0, unroll=4)
     row_id = lax.broadcasted_iota(jnp.int32, (128, 128), 0)
     for q in range(cols // 128):
-        spread[:, q * 128 : (q + 1) * 128] = jnp.where(row_id == q * GROUPS // (cols // 128), 1.0, 0.0).astype(jnp.bfloat16)
+        spread[:, q * 128 : (q + 1) * 128] = jnp.where(row_id == FIRST + q, 1.0, 0.0).astype(jnp.bfloat16)
     flags = bad[...]
     lane = lax.broadcasted_iota(jnp.int32, (BLOCK_ROWS, 128), 1)
     shift = jnp.minimum(lane, GROUPS)
@@ -158,7 +262,7 @@
         good = jnp.concatenate(rows, axis=0).astype(jnp.bfloat16)
         mask = jnp.dot(good, spread[...], preferred_element_type=jnp.float32).astype(jnp.bfloat16)
         part = pl.ds(k * group, group)
-        pltpu.make_async_copy(blocks.at[part], buf.at[part], sem_in.at[k]).wait()
+        pltpu.make_async_copy(blocks.at[part, :, pl.ds(skip, cols)], buf.at[part], sem_in.at[k]).wait()
         out[part] = buf[part] * mask.reshape(group, BLOCK_ROWS, cols)
         for n in range(k * group, (k + 1) * group):
             pltpu.make_async_copy(out.at[n], send.at[where[n]], sem_out).start()
@@ -167,6 +271,7 @@
 
 def pack(dest, flags, blocks, slots):
     count, _, cols = blocks.shape
+    cols = cols - cols // GROUPS * FIRST
     hbm = pl.BlockSpec(memory_space=pltpu.HBM)
     return pl.pallas_call(
         pack_kernel,
@@ -191,12 +296,30 @@
     )(*(pltpu.with_memory_space_constraint(item, pltpu.HBM) for item in (dest, flags, blocks)))
 
 
-def cover_kernel(meta, placing, spread, factor):
-    slots = meta.shape[0]
+def cover_kernel(got, placing, spread, factor, meta, sem):
+    sources = got.shape[0]
+    slots = sources * SLOT_CAP
+    label = pltpu.make_async_copy(got.at[:, pl.ds(got.shape[1] - META_ROWS, META_ROWS), :], meta, sem)
+    label.start()
+    label.wait()
     cols = spread.shape[1]
     lines = placing.shape[1]
     rows = placing.shape[0]
-    words = jnp.transpose(meta[...].astype(jnp.float32))
+    turned = jnp.transpose(meta[...].astype(jnp.float32).reshape(sources * META_ROWS, 128))
+    turned = turned[0:BLOCK_ROWS, :].astype(jnp.bfloat16)
+    meta_row = lax.broadcasted_iota(jnp.int32, (sources * META_ROWS, slots), 0)
+    meta_slot = lax.broadcasted_iota(jnp.int32, (sources * META_ROWS, slots), 1)
+    meta_base = meta_slot // SLOT_CAP * META_ROWS + meta_slot % SLOT_CAP * 4
+    low, high, begin = (
+        jnp.dot(
+            turned,
+            jnp.where(meta_row == meta_base + t, 1.0, 0.0).astype(jnp.bfloat16),
+            preferred_element_type=jnp.float32,
+        )
+        for t in range(3)
+    )
+    begin = jnp.broadcast_to(begin[0:1, :] + 256.0 * begin[1:2, :] - 1.0, (8, slots))
+    words = jnp.concatenate([low + 256.0 * high, begin], axis=0)
     slot_id = lax.broadcasted_iota(jnp.int32, (slots, lines), 0)
     line_id = lax.broadcasted_iota(jnp.int32, (slots, lines), 1)
     pick = jnp.where(slot_id == line_id // BLOCK_ROWS, 1.0, 0.0).astype(jnp.float32)
@@ -223,8 +346,9 @@
         ).astype(jnp.bfloat16)
 
 
-def cover(got_meta, row_count, cols):
-    slots = got_meta.shape[0]
+def cover(got, row_count, cols):
+    sources = got.shape[0]
+    slots = sources * SLOT_CAP
     vmem = pl.BlockSpec(memory_space=pltpu.VMEM)
     return pl.pallas_call(
         cover_kernel,
@@ -233,11 +357,12 @@
             jax.ShapeDtypeStruct((VISITS * row_count, cols), jnp.bfloat16),
             jax.ShapeDtypeStruct((VISITS * row_count, 128), jnp.float32),
         ),
-        in_specs=[vmem],
+        in_specs=[pl.BlockSpec(memory_space=pltpu.HBM)],
         out_specs=(vmem, vmem, vmem),
+        scratch_shapes=[pltpu.VMEM((sources, META_ROWS, 128), jnp.bfloat16), pltpu.SemaphoreType.DMA],
         compiler_params=params(24),
         name="coverage",
-    )(got_meta)
+    )(pltpu.with_memory_space_constraint(got, pltpu.HBM))
 
 
 def column_kernel(padded, table, out):
@@ -355,56 +480,121 @@
 PLACE_CHUNK = 512
 
 
-def place_kernel(got, placing, factor_hbm, source, table, science, sums, images, buf, acc, factor, sem_got, sem_img, sem_small):
+def scale_rows(summed, factor, first, group):
+    rows = summed.shape[0]
+    spread = jnp.concatenate(
+        [
+            jnp.broadcast_to(factor[:, first + q : first + q + 1], (rows, group))
+            for q in range(summed.shape[1] // group)
+        ],
+        axis=1,
+    )
+    return (summed * spread).astype(jnp.bfloat16)
+
+
+def correlate(value, images, lanes, rows, partial):
+    chunk = value.shape[1]
+    ones = jnp.ones((ONES_ROWS, chunk), jnp.bfloat16)
+    for t in range(rows // TILE):
+        left = jnp.concatenate(
+            [value[v * rows + t * TILE : v * rows + (t + 1) * TILE, :] for v in range(VISITS)], axis=0
+        )
+        right = images[:, t * TILE : t * TILE + SPAN, lanes].reshape(NPOW * SPAN, chunk)
+        right = jnp.concatenate([right, ones], axis=0)
+        product = lax.dot_general(left, right, (((1,), (1,)), ((), ())), preferred_element_type=jnp.float32)
+        partial = product if partial is None else partial + product
+    return partial
+
+
+def early_kernel(got, placing, factor, images, science, acc, buf, sem):
+    rows = science.shape[1]
+    copy = pltpu.make_async_copy(got.at[:, pl.ds(0, buf.shape[1]), :], buf, sem)
+    copy.start()
+    copy.wait()
+    columns = []
+    for q in range(FIRST):
+        ranks = [
+            buf[:, (r * FIRST + q) * BLOCK_ROWS : (r * FIRST + q + 1) * BLOCK_ROWS, :] for r in range(SLOT_CAP)
+        ]
+        columns.append(jnp.stack(ranks, axis=1).reshape(-1, 128))
+    right = jnp.concatenate(columns, axis=1)
+    summed = jnp.dot(placing[...], right, preferred_element_type=jnp.float32)
+    value = scale_rows(summed, factor, 0, 128)
+    for v in range(VISITS):
+        science[v, :, :] = value[v * rows : (v + 1) * rows, :]
+    acc[...] = correlate(value, images, slice(0, FIRST * 128), rows, None)
+
+
+def place_early(got, placing, factor, images, row_count):
+    sources = got.shape[0]
+    vmem = pl.BlockSpec(memory_space=pltpu.VMEM)
+    return pl.pallas_call(
+        early_kernel,
+        out_shape=(
+            jax.ShapeDtypeStruct((VISITS, row_count, FIRST * 128), jnp.bfloat16),
+            jax.ShapeDtypeStruct((VISITS * TILE, NPOW * SPAN + ONES_ROWS), jnp.float32),
+        ),
+        in_specs=[pl.BlockSpec(memory_space=pltpu.HBM), vmem, vmem, vmem],
+        out_specs=(vmem, vmem),
+        scratch_shapes=[
+            pltpu.VMEM((sources, SLOT_CAP * FIRST * BLOCK_ROWS, 128), jnp.bfloat16),
+            pltpu.SemaphoreType.DMA,
+        ],
+        compiler_params=params(28),
+        name="place_first_groups",
+    )(pltpu.with_memory_space_constraint(got, pltpu.HBM), placing, factor, images)
+
+
+def place_kernel(got, placing, factor_hbm, source, table_hbm, before_hbm, science, sums, images, buf, acc, factor, table, before, sem_got, sem_img, sem_small):
     rows = science.shape[1]
     cols = science.shape[2]
+    skip = source.shape[2] - cols
     chunk = PLACE_CHUNK
-    group = cols // GROUPS
-    small = pltpu.make_async_copy(factor_hbm, factor, sem_small)
+    group = source.shape[2] // GROUPS
+    small = pltpu.make_async_copy(factor_hbm, factor, sem_small.at[0])
     small.start()
+    later = [
+        pltpu.make_async_copy(before_hbm, before, sem_small.at[1]),
+        pltpu.make_async_copy(table_hbm, table, sem_small.at[2]),
+    ]
+    rest = pltpu.make_async_copy(source.at[:, :, pl.ds(0, skip)], images.at[:, :, pl.ds(0, skip)], sem_img.at[cols // chunk])
     copies = []
     for c in range(cols // chunk):
         lanes = slice(c * chunk, (c + 1) * chunk)
+        late = slice(skip + c * chunk, skip + (c + 1) * chunk)
         copies.append(
             (
                 pltpu.make_async_copy(got.at[:, :, lanes], buf.at[:, :, lanes], sem_got.at[c]),
-                pltpu.make_async_copy(source.at[:, :, lanes], images.at[:, :, lanes], sem_img.at[c]),
+                pltpu.make_async_copy(source.at[:, :, late], images.at[:, :, late], sem_img.at[c]),
             )
         )
-    for item in copies[0]:
-        item.start()
+    for pair in copies[:2]:
+        for item in pair:
+            item.start()
     partial = None
-    ones = jnp.ones((ONES_ROWS, chunk), jnp.bfloat16)
     for c in range(cols // chunk):
         lanes = slice(c * chunk, (c + 1) * chunk)
+        late = slice(skip + c * chunk, skip + (c + 1) * chunk)
         copies[c][0].wait()
-        if c + 1 < len(copies):
-            copies[c + 1][0].start()
+        if c + 2 < len(copies):
+            copies[c + 2][0].start()
         summed = jnp.dot(placing[...], buf[:, :, lanes].reshape(-1, chunk), preferred_element_type=jnp.float32)
         if c == 0:
             small.wait()
-        spread = jnp.concatenate(
-            [
-                jnp.broadcast_to(factor[:, q : q + 1], (VISITS * rows, group))
-                for q in range(c * chunk // group, (c + 1) * chunk // group)
-            ],
-            axis=1,
-        )
-        value = (summed * spread).astype(jnp.bfloat16)
+            for item in later:
+                item.start()
+        value = scale_rows(summed, factor, (skip + c * chunk) // group, group)
         for v in range(VISITS):
             science[v, :, lanes] = value[v * rows : (v + 1) * rows, :]
         copies[c][1].wait()
-        if c + 1 < len(copies):
-            copies[c + 1][1].start()
-        for t in range(rows // TILE):
-            left = jnp.concatenate(
-                [value[v * rows + t * TILE : v * rows + (t + 1) * TILE, :] for v in range(VISITS)], axis=0
-            )
-            right = images[:, t * TILE : t * TILE + SPAN, lanes].reshape(NPOW * SPAN, chunk)
-            right = jnp.concatenate([right, ones], axis=0)
-            product = lax.dot_general(left, right, (((1,), (1,)), ((), ())), preferred_element_type=jnp.float32)
-            partial = product if partial is None else partial + product
-    acc[...] = partial
+        if c + 2 < len(copies):
+            copies[c + 2][1].start()
+        if c == len(copies) - 2:
+            rest.start()
+        partial = correlate(value, images, late, rows, partial)
+    for item in later:
+        item.wait()
+    acc[...] = partial + before[...]
     row_id = lax.broadcasted_iota(jnp.int32, (32, 128), 0)
     lane_id = lax.broadcasted_iota(jnp.int32, (32, 128), 1)
     result = jnp.zeros((32, 128), jnp.float32)
@@ -420,9 +610,10 @@
         item = jnp.where(row_id == BASIS_COUNT, flat, item)
         result = result + jnp.where(lane_id == v, item, 0.0)
     sums[...] = result
-
-
-def place(got, placing, factor, images, bands, row_count):
+    rest.wait()
+
+
+def place(got, placing, factor, images, bands, before, row_count):
     slots, _, cols = got.shape
     table = jnp.asarray(bands)
     vmem = pl.BlockSpec(memory_space=pltpu.VMEM)
@@ -434,15 +625,17 @@
             jax.ShapeDtypeStruct((32, 128), jnp.float32),
             jax.ShapeDtypeStruct(images.shape, jnp.bfloat16),
         ),
-        in_specs=[hbm, vmem, hbm, hbm, vmem],
+        in_specs=[hbm, vmem, hbm, hbm, hbm, hbm],
         out_specs=(vmem, vmem, vmem),
         scratch_shapes=[
             pltpu.VMEM(got.shape, jnp.bfloat16),
             pltpu.VMEM((VISITS * TILE, NPOW * SPAN + ONES_ROWS), jnp.float32),
             pltpu.VMEM(factor.shape, jnp.float32),
+            pltpu.VMEM(table.shape, jnp.float32),
+            pltpu.VMEM(before.shape, jnp.float32),
             pltpu.SemaphoreType.DMA((cols // PLACE_CHUNK,)),
-            pltpu.SemaphoreType.DMA((cols // PLACE_CHUNK,)),
-            pltpu.SemaphoreType.DMA,
+            pltpu.SemaphoreType.DMA((cols // PLACE_CHUNK + 1,)),
+            pltpu.SemaphoreType.DMA((3,)),
         ],
         compiler_params=params(40),
         name="place_and_correlate",
@@ -451,13 +644,15 @@
         placing,
         pltpu.with_memory_space_constraint(factor, pltpu.HBM),
         pltpu.with_memory_space_constraint(images, pltpu.HBM),
-        table,
+        pltpu.with_memory_space_constraint(table, pltpu.HBM),
+        pltpu.with_memory_space_constraint(before, pltpu.HBM),
     )
 
 
-def model_kernel(sums, inverse, table, images, science, count, out, coeffs, wide, narrow, buf, sem):
+def model_kernel(sums, inverse, table, images, early, science, count, out, coeffs, wide, narrow, buf, sem):
     rows = science.shape[1]
-    cols = science.shape[2]
+    skip = early.shape[2]
+    cols = skip + science.shape[2]
     chunk = 256
     rhs = sums[0:32, :]
     for k in range(1, sums.shape[0] // 32):
@@ -486,15 +681,20 @@
                 full = model[v * TILE : (v + 1) * TILE, :] + level[v]
                 seen = count[v * rows + t * TILE : v * rows + (t + 1) * TILE, lanes]
                 weight = jnp.minimum(seen.astype(jnp.float32), 1.0)
-                buf[v, at, lanes] = (science[v, at, lanes].astype(jnp.float32) - weight * full).astype(jnp.bfloat16)
+                if (c + 1) * chunk <= skip:
+                    seen = early[v, at, lanes]
+                else:
+                    seen = science[v, at, c * chunk - skip : (c + 1) * chunk - skip]
+                buf[v, at, lanes] = (seen.astype(jnp.float32) - weight * full).astype(jnp.bfloat16)
         copies.append(pltpu.make_async_copy(buf.at[:, :, lanes], out.at[:, :, lanes], sem.at[c]))
         copies[-1].start()
     for item in copies:
         item.wait()
 
 
-def model(sums, inverse, images, science, count, bands):
+def model(sums, inverse, images, early, science, count, bands):
     _, rows, cols = science.shape
+    cols = cols + early.shape[2]
     table = jnp.asarray(bands)
     vmem = pl.BlockSpec(memory_space=pltpu.VMEM)
     return pl.pallas_call(
@@ -503,7 +703,7 @@
             pltpu.HBM((VISITS, rows, cols), jnp.bfloat16),
             jax.ShapeDtypeStruct((VISITS, TERMS), jnp.float32),
         ),
-        in_specs=[vmem] * 6,
+        in_specs=[vmem] * 7,
         out_specs=(pl.BlockSpec(memory_space=pltpu.HBM), vmem),
         scratch_shapes=[
             pltpu.VMEM((VISITS * TILE, NPOW * SPAN), jnp.float32),
@@ -513,7 +713,7 @@
         ],
         compiler_params=params(28),
         name="model_and_difference",
-    )(sums, inverse, table, images, science, count)
+    )(sums, inverse, table, images, early, science, count)
 
 
 def inverse_of(matrix):
@@ -542,25 +742,28 @@
     bands = row_bands(taps)
 
     flags = badmask.T
-    meta = describe(dest, offset, visit_id, flags, slots, row_count)
-    got_meta = lax.all_to_all(meta, axes, split_axis=0, concat_axis=0, tiled=True)
+    send_first = pack_first(dest, offset, visit_id, flags, blocks, sources, row_count)
+    send_first, rows = lax.optimization_barrier((send_first, template[0]))
+    got_first = lax.all_to_all(send_first, axes, split_axis=0, concat_axis=0, tiled=True)
+    got_first = pltpu.with_memory_space_constraint(got_first, pltpu.HBM)
     send = pack(dest, flags, blocks, slots)
-    send, got_meta, rows = lax.optimization_barrier((send, got_meta, template[0]))
-    got = lax.all_to_all(send, axes, split_axis=0, concat_axis=0, tiled=True)
-
     above, below = halo(rows)
     tall = jnp.concatenate([above, rows, below], axis=0)
     padded = jnp.pad(tall, ((0, 0), (HALF_TAPS, 128 - HALF_TAPS)))
     images = column_pass(padded, taps, cols)
-    placing, count, factor = cover(got_meta, row_count, cols)
+    send, got_first, images = lax.optimization_barrier((send, got_first, images))
+    got = lax.all_to_all(send, axes, split_axis=0, concat_axis=0, tiled=True)
+
+    placing, count, factor = cover(got_first, row_count, cols)
 
     shares = lax.all_gather(gram(images, count, taps), "visit", axis=0, tiled=False)
     normal = jnp.sum(shares, axis=0)
     inverse = jnp.pad(inverse_of(normal), ((0, 0), (0, 32 - TERMS), (0, 128 - TERMS)))
 
-    science, sums, images = place(got, placing, factor, images, bands, row_count)
+    early, before = place_early(got_first, placing, factor, images, row_count)
+    science, sums, images = place(got, placing, factor, images, bands, before, row_count)
     sums = lax.all_gather(sums, "visit", axis=0, tiled=True)
-    difference, coeffs = model(sums, inverse, images, science, count, bands)
+    difference, coeffs = model(sums, inverse, images, early, science, count, bands)
     return (difference[:, None], coeffs[:, None])
 
 

time: 134 us -> 133 us (level)
  blocking collectives: 27.8 us -> 10.9 us
  local copies, waits for them, and re-layouts: 1.71 us -> 14.8 us
  Pallas kernels: 54.5 us -> 57.5 us
  waiting for transfers between devices: 18.8 us -> 17.1 us
    all_gather x1, blocking collectives: 22.5 us -> 5.64 us  [body(): lax.all_gather(gram(images, count, taps), 'visit', axis=0, tiled=False)]
    unnamed x10 -> x24, local copies, waits for them, and re-layouts: 0.73 us -> 14 us
    all_to_all x1, waiting for transfers between devices: 15.4 us -> 4.35 us  [body(): got = lax.all_to_all(send, axes, split_axis=0, concat_axis=0, tiled=True)]
    all_to_all x1, waiting for transfers between devices: 3.45 us -> 12.7 us  [body(): lax.all_to_all(send_first, axes, split_axis=0, concat_axis=0, tiled=True)]
    pallas_call x1 -> x2, Pallas kernels: 1.61 us -> 5.67 us  [the longest x1 3.07 us: place_early(): pl.pallas_call(early_kernel, out_shape=(jax.ShapeDtypeStruct((VISITS, row...]
    pallas_call x1, Pallas kernels: 9.69 us -> 8.04 us  [place(): pl.pallas_call(place_kernel, out_shape=(jax.ShapeDtypeStruct((VISITS, row...]
  transfers between devices with their start and end apart: 4 -> 4, of which waited for: 2 -> 2; matrix products, arithmetic and copies ran while one was open for 12% -> 12% of each run, Pallas kernels for 29% -> 33%
where the time goes in v3:
time: 133 us; the launch traced here: 132 us
  Pallas kernels  57.5 us (43%)
  waiting for transfers between devices  17.1 us (13%)
  starting transfers between devices  15.6 us (12%)
  local copies, waits for them, and re-layouts  14.8 us (11%)
  other arithmetic  14.5 us (11%)
  blocking collectives  10.9 us (8%)
    pallas_call x1, Pallas kernels, gram(): pl.pallas_call(gram_kernel, out_shape=jax.ShapeDtypeStruct((VISITS, TERMS...  31.3 us
    unnamed x24, local copies, waits for them, and re-layouts  14 us
    all_to_all x1, waiting for transfers between devices, body(): lax.all_to_all(send_first, axes, split_axis=0, concat_axis=0, tiled=True)  12.7 us
    pallas_call x1, Pallas kernels, place(): pl.pallas_call(place_kernel, out_shape=(jax.ShapeDtypeStruct((VISITS, row...  8.04 us
    all_to_all x1, starting transfers between devices, body(): lax.all_to_all(send_first, axes, split_axis=0, concat_axis=0, tiled=True)  7.32 us
    another operation x4, other arithmetic, inverse_of(): lower = jnp.linalg.cholesky(matrix)  6.74 us
    another operation x3, other arithmetic, inverse_of(): half = jax.scipy.linalg.solve_triangular(lower, eye, lower=True)  5.79 us
    all_gather x1, blocking collectives, body(): lax.all_gather(gram(images, count, taps), 'visit', axis=0, tiled=False)  5.64 us
  transfers between devices with their start and end apart: 4, of which 2 were waited for; matrix products, arithmetic and copies ran while one was open for 12% of the time, Pallas kernels for 33%

profile of v3, /device:TPU:0, one launch (start us, length us, event | category | flops | bytes accessed | tf_op | source)
XLA Modules:
  0.0 131.9 jit_solution(10119984994394656494)
XLA Ops:
  0.6 2.6 %pack_first_groups.1 = bf16[32,136,128]{2,1,0:T(8,128)(2,1)} custom-call(s32[1,32]{1,0:T(1,128)} %bitcast.28, s32[1,32]{1,0:T(1,128)} %bitcast.29, s32[1,32]{1,0:T(1,128)} %bitcast.30, s32[16,32]{1,0:T(8,128)} %bitcast.26, s32[32]{0:T(128)} %refs_4_.1, bf16[32,16,2048]{2,1,0:T(8,128)(2,1)} %refs_5_.1), custom_call_target="tpu_custom_call" | custom-call | tf_op jit(solution)/shard_map/pack_first_groups/pallas_call | solution.py:176
  3.2 7.3 %all-to-all-start = ((bf16[32,136,128]{2,1,0:T(8,128)(2,1)}), bf16[32,136,128]{2,1,0:T(8,128)(2,1)S(1)}, u32[]{:S(2)}, u32[]{:S(2)}) async-start(bf16[32,136,128]{2,1,0:T(8,128)(2,1)} %pack_first_groups.1), calls=%async_computation | async-start | bytes 2228224 | tf_op jit(solution)/shard_map/all_to_all | solution.py:747
  10.6 1.3 collective-permute-start.1
  11.9 3.0 %collective-permute-start = (bf16[16,2048]{1,0:T(8,128)(2,1)S(1)}, bf16[16,2048]{1,0:T(8,128)(2,1)S(1)}, u32[]{:S(2)}, u32[]{:S(2)}) collective-permute-start(bf16[16,2048]{1,0:T(8,128)(2,1)S(1)} %get-tuple-element.38), channel_id=1, source_target_pairs={{0,1},{1,2},{2,3},{4,5},{5,6},{6,7},{8,9},{9,10},{10,11},{12,13},{... | collective-permute-start | bytes 196616 | tf_op jit(solution)/shard_map/ppermute | solution.py:730
  14.9 3.4 %pack_blocks.1 = bf16[64,16,1536]{2,1,0:T(8,128)(2,1)} custom-call(s32[32]{0:T(128)} %refs_4_.1, s32[16,32]{1,0:T(8,128)} %bitcast.27, bf16[32,16,2048]{2,1,0:T(8,128)(2,1)} %refs_5_.1), custom_call_target="tpu_custom_call" | custom-call | tf_op jit(solution)/shard_map/pack_blocks/pallas_call | solution.py:276
  19.4 2.9 %column_pass.1.images.source = bf16[7,288,2048]{2,1,0:T(8,128)(2,1)S(1)} custom-call(bf16[288,2176]{1,0:T(8,128)(2,1)S(1)} %fusion.5.padded, bf16[256,896]{1,0:T(8,128)(2,1)S(1)} %copy-done.7), custom_call_target="tpu_custom_call" | custom-call | tf_op jit(solution)/shard_map/column_pass/pallas_call | solution.py:380
  22.3 3.2 %copy-done = bf16[7,288,2048]{2,1,0:T(8,128)(2,1)} copy-done((bf16[7,288,2048]{2,1,0:T(8,128)(2,1)}, bf16[7,288,2048]{2,1,0:T(8,128)(2,1)S(1)}, u32[]{:S(2)}) %copy-start) | copy-done | bytes 8257560
  25.5 12.7 %all-to-all-done.got = bf16[32,136,128]{2,1,0:T(8,128)(2,1)S(1)} async-done(((bf16[32,136,128]{2,1,0:T(8,128)(2,1)}), bf16[32,136,128]{2,1,0:T(8,128)(2,1)S(1)}, u32[]{:S(2)}, u32[]{:S(2)}) %all-to-all-start) | async-done | bytes 1114144 | tf_op jit(solution)/shard_map/all_to_all | solution.py:747
  38.2 1.0 copy-done.10
  39.2 3.9 %all-to-all-start.1 = ((bf16[64,16,1536]{2,1,0:T(8,128)(2,1)}), bf16[64,16,1536]{2,1,0:T(8,128)(2,1)}, u32[]{:S(2)}, u32[]{:S(2)}) async-start(bf16[64,16,1536]{2,1,0:T(8,128)(2,1)} %pack_blocks.1), calls=%async_computation.1 | async-start | bytes 6291456 | tf_op jit(solution)/shard_map/all_to_all | solution.py:755
  44.3 2.4 %coverage.1 = (bf16[512,1024]{1,0:T(8,128)(2,1)S(1)}, bf16[512,2048]{1,0:T(8,128)(2,1)S(1)}, f32[512,128]{1,0:T(8,128)S(1)}) custom-call(bf16[32,136,128]{2,1,0:T(8,128)(2,1)} %copy-done.10), custom_call_target="tpu_custom_call" | custom-call | tf_op jit(solution)/shard_map/coverage/pallas_call | solution.py:353
  46.8 3.4 %copy-done.1 = bf16[7,288,2048]{2,1,0:T(8,128)(2,1)S(1)} copy-done((bf16[7,288,2048]{2,1,0:T(8,128)(2,1)S(1)}, bf16[7,288,2048]{2,1,0:T(8,128)(2,1)}, u32[]{:S(2)}) %copy-start.1) | copy-done | bytes 8257560
  50.2 1.0 copy-done.8
  51.2 31.3 %normal_matrix.1 = f32[2,29,29]{2,1,0:T(8,128)S(1)} custom-call(bf16[7,288,2048]{2,1,0:T(8,128)(2,1)S(1)} %copy-done.1, bf16[1792,96]{1,0:T(8,128)(2,1)S(1)} %copy-done.8, bf16[512,2048]{1,0:T(8,128)(2,1)S(1)} %get-tuple-element.26.count), custom_call_target="tpu_custom_call" | custom-call | tf_op jit(solution)/shard_map/normal_matrix/pallas_call | solution.py:465
  82.6 5.6 %all-gather = f32[8,29,29]{2,1,0:T(8,128)S(1)} all-gather(f32[2,29,29]{2,1,0:T(8,128)S(1)} %normal_matrix.1), channel_id=2, replica_groups=mesh['patch'=8,'visit'=4] {'visit'}, dimensions={0}, use_global_device_ids=true | all-gather | bytes 33640 | tf_op jit(solution)/shard_map/all_gather | solution.py:759
  88.8 0.9 copy.19
  90.5 5.3 %custom-call.8 = f32[2,29,29]{2,1,0:T(8,128)S(1)} custom-call(f32[2,29,29]{2,1,0:T(8,128)S(1)} %fusion.8), custom_call_target="Cholesky" | custom-call | tf_op jit(solution)/shard_map/jit(cholesky)/cholesky | solution.py:721
  97.3 4.4 %custom-call.9 = f32[2,1,29,29]{2,3,1,0:T(8,128)S(1)} custom-call(f32[2,1,29,29]{3,2,1,0:T(8,128)S(1)} %select_bitcast_fusion), custom_call_target="InvertDiagBlocksLowerTriangular" | custom-call | tf_op jit(solution)/shard_map/jit(_solve_triangular)/vmap()/triangular_solve | solution.py:722
  102.3 3.3 %copy-done.2 = bf16[7,288,2048]{2,1,0:T(8,128)(2,1)S(1)} copy-done((bf16[7,288,2048]{2,1,0:T(8,128)(2,1)S(1)}, bf16[7,288,2048]{2,1,0:T(8,128)(2,1)}, u32[]{:S(2)}) %copy-start.2) | copy-done | bytes 8257560
  105.7 3.1 %place_first_groups.1 = (bf16[2,256,512]{2,1,0:T(8,128)(2,1)S(1)}, f32[128,688]{1,0:T(8,128)S(1)}) custom-call(bf16[32,136,128]{2,1,0:T(8,128)(2,1)} %copy-done.10, bf16[512,1024]{1,0:T(8,128)(2,1)S(1)} %get-tuple-element.21.placing, f32[512,128]{1,0:T(8,128)S(1)} %get-tuple-element.22.factor.factor_hbm, bf16[7,288,2048]{2,1,0:T(8,128)(2,1)S(1)} %copy-done.2), custom_call_target="tpu_custom_call" | custom-call | tf_op jit(solution)/shard_map/place_first_groups/pallas_call | solution.py:531
  110.3 4.3 %all-to-all-done.1.got = bf16[64,16,1536]{2,1,0:T(8,128)(2,1)} async-done(((bf16[64,16,1536]{2,1,0:T(8,128)(2,1)}), bf16[64,16,1536]{2,1,0:T(8,128)(2,1)}, u32[]{:S(2)}, u32[]{:S(2)}) %all-to-all-start.1) | async-done | bytes 3145760 | tf_op jit(solution)/shard_map/all_to_all | solution.py:755
  114.7 8.0 %place_and_correlate.1 = (bf16[2,256,1536]{2,1,0:T(8,128)(2,1)S(1)}, f32[32,128]{1,0:T(8,128)S(1)}, bf16[7,288,2048]{2,1,0:T(8,128)(2,1)S(1)}) custom-call(bf16[64,16,1536]{2,1,0:T(8,128)(2,1)} %all-to-all-done.1.got, bf16[512,1024]{1,0:T(8,128)(2,1)S(1)} %get-tuple-element.21.placing, f32[512,128]{1,0:T(8,128)} %copy-done.3, bf16[7,288,2048]{2,1,0:T(8,128)(2,1)} %copy-done, ...), custom_call_target="tpu_custom_call" | custom-call | tf_op jit(solution)/shard_map/place_and_correlate/pallas_call | solution.py:621
  122.7 5.2 %all_gather.9.sums = f32[128,128]{1,0:T(8,128)S(1)} all-gather(f32[32,128]{1,0:T(8,128)S(1)} %get-tuple-element.25), channel_id=1, replica_groups=mesh['patch'=8,'visit'=4] {'visit'}, dimensions={0}, use_global_device_ids=true | all-gather | bytes 81920 | tf_op jit(solution)/shard_map/all_gather | solution.py:765
  128.0 3.8 %model_and_difference.1 = (bf16[2,256,2048]{2,1,0:T(8,128)(2,1)}, f32[2,29]{1,0:T(2,128)}) custom-call(f32[128,128]{1,0:T(8,128)S(1)} %all_gather.9.sums, f32[2,32,128]{2,1,0:T(8,128)S(1)} %pad.9.inverse, f32[7,64,96]{2,1,0:T(8,128)S(1)} %copy-done.4, bf16[7,288,2048]{2,1,0:T(8,128)(2,1)S(1)} %get-tuple-element.27.images, ...), custom_call_target="tpu_custom_call" | custom-call | tf_op jit(solution)/shard_map/model_and_difference/pallas_call | solution.py:700
  (34 shorter events, 7.3 us)
Async XLA Ops:
  0.6 9.9 %copy-start.11 = (bf16[1,256,2048]{2,1,0:T(8,128)(2,1)S(1)}, bf16[1,256,2048]{2,1,0:T(8,128)(2,1)}, u32[]{:S(2)}) copy-start(bf16[1,256,2048]{2,1,0:T(8,128)(2,1)} %param.9) | copy-start | bytes 3145732
  3.2 35.0 %all-to-all-start = ((bf16[32,136,128]{2,1,0:T(8,128)(2,1)}), bf16[32,136,128]{2,1,0:T(8,128)(2,1)S(1)}, u32[]{:S(2)}, u32[]{:S(2)}) async-start(bf16[32,136,128]{2,1,0:T(8,128)(2,1)} %pack_first_groups.1), calls=%async_computation | async-start | bytes 2228224 | tf_op jit(solution)/shard_map/all_to_all | solution.py:747
  10.6 7.7 %collective-permute-start.1 = (bf16[16,2048]{1,0:T(8,128)(2,1)S(1)}, bf16[16,2048]{1,0:T(8,128)(2,1)S(1)}, u32[]{:S(2)}, u32[]{:S(2)}) collective-permute-start(bf16[16,2048]{1,0:T(8,128)(2,1)S(1)} %get-tuple-element.39), channel_id=1, source_target_pairs={{1,0},{2,1},{3,2},{5,4},{6,5},{7,6},{9,8},{10,9},{11,10},{13,12},{... | collective-permute-start | bytes 196616 | tf_op jit(solution)/shard_map/ppermute | solution.py:731
  11.9 6.5 %collective-permute-start = (bf16[16,2048]{1,0:T(8,128)(2,1)S(1)}, bf16[16,2048]{1,0:T(8,128)(2,1)S(1)}, u32[]{:S(2)}, u32[]{:S(2)}) collective-permute-start(bf16[16,2048]{1,0:T(8,128)(2,1)S(1)} %get-tuple-element.38), channel_id=1, source_target_pairs={{0,1},{1,2},{2,3},{4,5},{5,6},{6,7},{8,9},{9,10},{10,11},{12,13},{... | collective-permute-start | bytes 196616 | tf_op jit(solution)/shard_map/ppermute | solution.py:730
  18.3 1.0 copy-start.7
  22.3 3.2 %copy-start = (bf16[7,288,2048]{2,1,0:T(8,128)(2,1)}, bf16[7,288,2048]{2,1,0:T(8,128)(2,1)S(1)}, u32[]{:S(2)}) copy-start(bf16[7,288,2048]{2,1,0:T(8,128)(2,1)S(1)} %column_pass.1.images.source) | copy-start | bytes 24772612
  38.2 1.0 copy-start.10
  39.2 75.5 %all-to-all-start.1 = ((bf16[64,16,1536]{2,1,0:T(8,128)(2,1)}), bf16[64,16,1536]{2,1,0:T(8,128)(2,1)}, u32[]{:S(2)}, u32[]{:S(2)}) async-start(bf16[64,16,1536]{2,1,0:T(8,128)(2,1)} %pack_blocks.1), calls=%async_computation.1 | async-start | bytes 6291456 | tf_op jit(solution)/shard_map/all_to_all | solution.py:755
  46.8 55.6 %copy-start.3 = (f32[512,128]{1,0:T(8,128)}, f32[512,128]{1,0:T(8,128)S(1)}, u32[]{:S(2)}) copy-start(f32[512,128]{1,0:T(8,128)S(1)} %get-tuple-element.22.factor.factor_hbm) | copy-start | bytes 786436
  46.8 3.4 %copy-start.1 = (bf16[7,288,2048]{2,1,0:T(8,128)(2,1)S(1)}, bf16[7,288,2048]{2,1,0:T(8,128)(2,1)}, u32[]{:S(2)}) copy-start(bf16[7,288,2048]{2,1,0:T(8,128)(2,1)} %copy-done) | copy-start | bytes 24772612
  50.2 1.0 copy-start.8
  102.3 3.3 %copy-start.2 = (bf16[7,288,2048]{2,1,0:T(8,128)(2,1)S(1)}, bf16[7,288,2048]{2,1,0:T(8,128)(2,1)}, u32[]{:S(2)}) copy-start(bf16[7,288,2048]{2,1,0:T(8,128)(2,1)} %copy-done) | copy-start | bytes 24772612
  108.8 0.8 copy-start.5
  109.5 0.8 copy-start.9
  114.7 13.3 %copy-start.4 = (f32[7,64,96]{2,1,0:T(8,128)S(1)}, f32[7,64,96]{2,1,0:T(8,128)}, u32[]{:S(2)}) copy-start(f32[7,64,96]{2,1,0:T(8,128)} %constant.58.clone.table_hbm.table) | copy-start | bytes 516100
  114.7 13.3 %copy-start.6 = (bf16[2,256,512]{2,1,0:T(8,128)(2,1)S(1)}, bf16[2,256,512]{2,1,0:T(8,128)(2,1)}, u32[]{:S(2)}) copy-start(bf16[2,256,512]{2,1,0:T(8,128)(2,1)} %copy-done.5) | copy-start | bytes 1572868

commit v4 on v3

--- a/solution.py
+++ b/solution.py
@@ -357,12 +357,12 @@
             jax.ShapeDtypeStruct((VISITS * row_count, cols), jnp.bfloat16),
             jax.ShapeDtypeStruct((VISITS * row_count, 128), jnp.float32),
         ),
-        in_specs=[pl.BlockSpec(memory_space=pltpu.HBM)],
+        in_specs=[pl.BlockSpec(memory_space=pl.ANY)],
         out_specs=(vmem, vmem, vmem),
         scratch_shapes=[pltpu.VMEM((sources, META_ROWS, 128), jnp.bfloat16), pltpu.SemaphoreType.DMA],
         compiler_params=params(24),
         name="coverage",
-    )(pltpu.with_memory_space_constraint(got, pltpu.HBM))
+    )(got)
 
 
 def column_kernel(padded, table, out):
@@ -534,7 +534,7 @@
             jax.ShapeDtypeStruct((VISITS, row_count, FIRST * 128), jnp.bfloat16),
             jax.ShapeDtypeStruct((VISITS * TILE, NPOW * SPAN + ONES_ROWS), jnp.float32),
         ),
-        in_specs=[pl.BlockSpec(memory_space=pltpu.HBM), vmem, vmem, vmem],
+        in_specs=[pl.BlockSpec(memory_space=pl.ANY), vmem, vmem, vmem],
         out_specs=(vmem, vmem),
         scratch_shapes=[
             pltpu.VMEM((sources, SLOT_CAP * FIRST * BLOCK_ROWS, 128), jnp.bfloat16),
@@ -542,7 +542,7 @@
         ],
         compiler_params=params(28),
         name="place_first_groups",
-    )(pltpu.with_memory_space_constraint(got, pltpu.HBM), placing, factor, images)
+    )(got, placing, factor, images)
 
 
 def place_kernel(got, placing, factor_hbm, source, table_hbm, before_hbm, science, sums, images, buf, acc, factor, table, before, sem_got, sem_img, sem_small):
@@ -745,7 +745,6 @@
     send_first = pack_first(dest, offset, visit_id, flags, blocks, sources, row_count)
     send_first, rows = lax.optimization_barrier((send_first, template[0]))
     got_first = lax.all_to_all(send_first, axes, split_axis=0, concat_axis=0, tiled=True)
-    got_first = pltpu.with_memory_space_constraint(got_first, pltpu.HBM)
     send = pack(dest, flags, blocks, slots)
     above, below = halo(rows)
     tall = jnp.concatenate([above, rows, below], axis=0)
@@ -756,11 +755,12 @@
 
     placing, count, factor = cover(got_first, row_count, cols)
 
+    early, before = place_early(got_first, placing, factor, images, row_count)
+    images, before = lax.optimization_barrier((images, before))
     shares = lax.all_gather(gram(images, count, taps), "visit", axis=0, tiled=False)
     normal = jnp.sum(shares, axis=0)
     inverse = jnp.pad(inverse_of(normal), ((0, 0), (0, 32 - TERMS), (0, 128 - TERMS)))
 
-    early, before = place_early(got_first, placing, factor, images, row_count)
     science, sums, images = place(got, placing, factor, images, bands, before, row_count)
     sums = lax.all_gather(sums, "visit", axis=0, tiled=True)
     difference, coeffs = model(sums, inverse, images, early, science, count, bands)

time: 133 us -> 131 us (0.985)
  waiting for transfers between devices: 17.1 us -> 27.5 us
  local copies, waits for them, and re-layouts: 14.8 us -> 9.19 us
  other arithmetic: 14.5 us -> 10.6 us
  Pallas kernels: 57.5 us -> 55.6 us
    all_to_all x1, waiting for transfers between devices: 4.35 us -> 14.8 us  [body(): got = lax.all_to_all(send, axes, split_axis=0, concat_axis=0, tiled=True)]
    unnamed x24 -> x26, local copies, waits for them, and re-layouts: 14 us -> 9.07 us
  transfers between devices with their start and end apart: 4 -> 4, of which waited for: 2 -> 2; matrix products, arithmetic and copies ran while one was open for 12% -> 9% of each run, Pallas kernels for 33% -> 31%
where the time goes in v4:
time: 131 us
  Pallas kernels  55.6 us (42%)
  waiting for transfers between devices  27.5 us (21%)
  starting transfers between devices  15.5 us (12%)
  blocking collectives  10.9 us (8%)
  other arithmetic  10.6 us (8%)
  local copies, waits for them, and re-layouts  9.19 us (7%)
    pallas_call x1, Pallas kernels, gram(): pl.pallas_call(gram_kernel, out_shape=jax.ShapeDtypeStruct((VISITS, TERMS...  31.3 us
    all_to_all x1, waiting for transfers between devices, body(): got = lax.all_to_all(send, axes, split_axis=0, concat_axis=0, tiled=True)  14.8 us
    all_to_all x1, waiting for transfers between devices, body(): lax.all_to_all(send_first, axes, split_axis=0, concat_axis=0, tiled=True)  12.7 us
    unnamed x26, local copies, waits for them, and re-layouts  9.07 us
    pallas_call x1, Pallas kernels, place(): pl.pallas_call(place_kernel, out_shape=(jax.ShapeDtypeStruct((VISITS, row...  8.03 us
    all_to_all x1, starting transfers between devices, body(): lax.all_to_all(send_first, axes, split_axis=0, concat_axis=0, tiled=True)  7.29 us
    all_gather x1, blocking collectives, body(): lax.all_gather(gram(images, count, taps), 'visit', axis=0, tiled=False)  5.65 us
    another operation x4, other arithmetic, inverse_of(): lower = jnp.linalg.cholesky(matrix)  5.47 us
  transfers between devices with their start and end apart: 4, of which 2 were waited for; matrix products, arithmetic and copies ran while one was open for 9% of the time, Pallas kernels for 31%

profile of v4, /device:TPU:0, one launch (start us, length us, event | category | flops | bytes accessed | tf_op | source)
XLA Modules:
  0.0 130.9 jit_solution(2157704746303972946)
XLA Ops:
  0.6 2.6 %pack_first_groups.1 = bf16[32,136,128]{2,1,0:T(8,128)(2,1)} custom-call(s32[1,32]{1,0:T(1,128)} %bitcast.28, s32[1,32]{1,0:T(1,128)} %bitcast.29, s32[1,32]{1,0:T(1,128)} %bitcast.30, s32[16,32]{1,0:T(8,128)} %bitcast.26, s32[32]{0:T(128)} %refs_4_.1, bf16[32,16,2048]{2,1,0:T(8,128)(2,1)} %refs_5_.1), custom_call_target="tpu_custom_call" | custom-call | tf_op jit(solution)/shard_map/pack_first_groups/pallas_call | solution.py:176
  3.3 7.3 %all-to-all-start = ((bf16[32,136,128]{2,1,0:T(8,128)(2,1)}), bf16[32,136,128]{2,1,0:T(8,128)(2,1)S(1)}, u32[]{:S(2)}, u32[]{:S(2)}) async-start(bf16[32,136,128]{2,1,0:T(8,128)(2,1)} %pack_first_groups.1), calls=%async_computation | async-start | bytes 2228224 | tf_op jit(solution)/shard_map/all_to_all | solution.py:747
  10.6 1.3 collective-permute-start.1
  11.9 3.0 %collective-permute-start = (bf16[16,2048]{1,0:T(8,128)(2,1)S(1)}, bf16[16,2048]{1,0:T(8,128)(2,1)S(1)}, u32[]{:S(2)}, u32[]{:S(2)}) collective-permute-start(bf16[16,2048]{1,0:T(8,128)(2,1)S(1)} %get-tuple-element.42), channel_id=1, source_target_pairs={{0,1},{1,2},{2,3},{4,5},{5,6},{6,7},{8,9},{9,10},{10,11},{12,13},{... | collective-permute-start | bytes 196616 | tf_op jit(solution)/shard_map/ppermute | solution.py:730
  14.9 3.4 %pack_blocks.1 = bf16[64,16,1536]{2,1,0:T(8,128)(2,1)} custom-call(s32[32]{0:T(128)} %refs_4_.1, s32[16,32]{1,0:T(8,128)} %bitcast.27, bf16[32,16,2048]{2,1,0:T(8,128)(2,1)} %refs_5_.1), custom_call_target="tpu_custom_call" | custom-call | tf_op jit(solution)/shard_map/pack_blocks/pallas_call | solution.py:276
  18.4 0.5 fusion.5.padded
  18.9 0.4 copy-done.9
  19.3 2.9 %column_pass.1.images.source = bf16[7,288,2048]{2,1,0:T(8,128)(2,1)S(1)} custom-call(bf16[288,2176]{1,0:T(8,128)(2,1)S(1)} %fusion.5.padded, bf16[256,896]{1,0:T(8,128)(2,1)S(1)} %copy-done.9), custom_call_target="tpu_custom_call" | custom-call | tf_op jit(solution)/shard_map/column_pass/pallas_call | solution.py:380
  22.3 3.2 %copy-done = bf16[7,288,2048]{2,1,0:T(8,128)(2,1)} copy-done((bf16[7,288,2048]{2,1,0:T(8,128)(2,1)}, bf16[7,288,2048]{2,1,0:T(8,128)(2,1)S(1)}, u32[]{:S(2)}) %copy-start) | copy-done | bytes 8257560
  25.5 12.7 %all-to-all-done.got = bf16[32,136,128]{2,1,0:T(8,128)(2,1)S(1)} async-done(((bf16[32,136,128]{2,1,0:T(8,128)(2,1)}), bf16[32,136,128]{2,1,0:T(8,128)(2,1)S(1)}, u32[]{:S(2)}, u32[]{:S(2)}) %all-to-all-start) | async-done | bytes 1114144 | tf_op jit(solution)/shard_map/all_to_all | solution.py:747
  38.2 3.9 %all-to-all-start.1 = ((bf16[64,16,1536]{2,1,0:T(8,128)(2,1)}), bf16[64,16,1536]{2,1,0:T(8,128)(2,1)}, u32[]{:S(2)}, u32[]{:S(2)}) async-start(bf16[64,16,1536]{2,1,0:T(8,128)(2,1)} %pack_blocks.1), calls=%async_computation.1 | async-start | bytes 6291456 | tf_op jit(solution)/shard_map/all_to_all | solution.py:754
  42.2 1.6 %coverage.1 = (bf16[512,1024]{1,0:T(8,128)(2,1)S(1)}, bf16[512,2048]{1,0:T(8,128)(2,1)S(1)}, f32[512,128]{1,0:T(8,128)S(1)}) custom-call(bf16[32,136,128]{2,1,0:T(8,128)(2,1)S(1)} %all-to-all-done.got), custom_call_target="tpu_custom_call" | custom-call | tf_op jit(solution)/shard_map/coverage/pallas_call | solution.py:353
  43.8 3.8 %copy-done.1 = bf16[7,288,2048]{2,1,0:T(8,128)(2,1)S(1)} copy-done((bf16[7,288,2048]{2,1,0:T(8,128)(2,1)S(1)}, bf16[7,288,2048]{2,1,0:T(8,128)(2,1)}, u32[]{:S(2)}) %copy-start.1) | copy-done | bytes 8257560
  47.6 1.9 %place_first_groups.1 = (bf16[2,256,512]{2,1,0:T(8,128)(2,1)S(1)}, f32[128,688]{1,0:T(8,128)S(1)}) custom-call(bf16[32,136,128]{2,1,0:T(8,128)(2,1)S(1)} %all-to-all-done.got, bf16[512,1024]{1,0:T(8,128)(2,1)S(1)} %get-tuple-element.23.placing, f32[512,128]{1,0:T(8,128)S(1)} %get-tuple-element.24.factor.factor_hbm, bf16[7,288,2048]{2,1,0:T(8,128)(2,1)S(1)} %copy-done.1), custom_call_target="tpu_custom_call" | custom-call | tf_op jit(solution)/shard_map/place_first_groups/pallas_call | solution.py:531
  49.6 0.8 copy-done.7
  50.4 0.8 copy-done.2
  51.2 31.3 %normal_matrix.1 = f32[2,29,29]{2,1,0:T(8,128)S(1)} custom-call(bf16[7,288,2048]{2,1,0:T(8,128)(2,1)S(1)} %copy-done.2, bf16[1792,96]{1,0:T(8,128)(2,1)S(1)} %copy-done.10, bf16[512,2048]{1,0:T(8,128)(2,1)S(1)} %get-tuple-element.30.count), custom_call_target="tpu_custom_call" | custom-call | tf_op jit(solution)/shard_map/normal_matrix/pallas_call | solution.py:465
  82.5 5.6 %all-gather = f32[8,29,29]{2,1,0:T(8,128)S(1)} all-gather(f32[2,29,29]{2,1,0:T(8,128)S(1)} %normal_matrix.1), channel_id=2, replica_groups=mesh['patch'=8,'visit'=4] {'visit'}, dimensions={0}, use_global_device_ids=true | all-gather | bytes 33640 | tf_op jit(solution)/shard_map/all_gather | solution.py:760
  88.3 5.3 %custom-call.8 = f32[2,29,29]{2,1,0:T(8,128)S(1)} custom-call(f32[2,29,29]{2,1,0:T(8,128)S(1)} %fusion.8), custom_call_target="Cholesky" | custom-call | tf_op jit(solution)/shard_map/jit(cholesky)/cholesky | solution.py:721
  93.8 4.5 %custom-call.9 = f32[2,1,29,29]{2,3,1,0:T(8,128)S(1)} custom-call(f32[2,1,29,29]{3,2,1,0:T(8,128)S(1)} %select_bitcast_fusion), custom_call_target="InvertDiagBlocksLowerTriangular" | custom-call | tf_op jit(solution)/shard_map/jit(_solve_triangular)/vmap()/triangular_solve | solution.py:722
  98.8 14.8 %all-to-all-done.1.got = bf16[64,16,1536]{2,1,0:T(8,128)(2,1)} async-done(((bf16[64,16,1536]{2,1,0:T(8,128)(2,1)}), bf16[64,16,1536]{2,1,0:T(8,128)(2,1)}, u32[]{:S(2)}, u32[]{:S(2)}) %all-to-all-start.1) | async-done | bytes 3145760 | tf_op jit(solution)/shard_map/all_to_all | solution.py:754
  113.7 8.0 %place_and_correlate.1 = (bf16[2,256,1536]{2,1,0:T(8,128)(2,1)S(1)}, f32[32,128]{1,0:T(8,128)S(1)}, bf16[7,288,2048]{2,1,0:T(8,128)(2,1)S(1)}) custom-call(bf16[64,16,1536]{2,1,0:T(8,128)(2,1)} %all-to-all-done.1.got, bf16[512,1024]{1,0:T(8,128)(2,1)S(1)} %copy-done.4, f32[512,128]{1,0:T(8,128)} %copy-done.5, bf16[7,288,2048]{2,1,0:T(8,128)(2,1)} %copy-done, ...), custom_call_target="tpu_custom_call" | custom-call | tf_op jit(solution)/shard_map/place_and_correlate/pallas_call | solution.py:621
  121.7 5.2 %all_gather.9.sums = f32[128,128]{1,0:T(8,128)S(1)} all-gather(f32[32,128]{1,0:T(8,128)S(1)} %get-tuple-element.29), channel_id=1, replica_groups=mesh['patch'=8,'visit'=4] {'visit'}, dimensions={0}, use_global_device_ids=true | all-gather | bytes 81920 | tf_op jit(solution)/shard_map/all_gather | solution.py:765
  127.0 3.8 %model_and_difference.1 = (bf16[2,256,2048]{2,1,0:T(8,128)(2,1)}, f32[2,29]{1,0:T(2,128)}) custom-call(f32[128,128]{1,0:T(8,128)S(1)} %all_gather.9.sums, f32[2,32,128]{2,1,0:T(8,128)S(1)} %pad.9.inverse, f32[7,64,96]{2,1,0:T(8,128)S(1)} %copy-done.6, bf16[7,288,2048]{2,1,0:T(8,128)(2,1)S(1)} %get-tuple-element.31.images, ...), custom_call_target="tpu_custom_call" | custom-call | tf_op jit(solution)/shard_map/model_and_difference/pallas_call | solution.py:700
  (36 shorter events, 1.0 us)
Async XLA Ops:
  0.6 9.9 %copy-start.12 = (bf16[1,256,2048]{2,1,0:T(8,128)(2,1)S(1)}, bf16[1,256,2048]{2,1,0:T(8,128)(2,1)}, u32[]{:S(2)}) copy-start(bf16[1,256,2048]{2,1,0:T(8,128)(2,1)} %param.9) | copy-start | bytes 3145732
  3.3 34.9 %all-to-all-start = ((bf16[32,136,128]{2,1,0:T(8,128)(2,1)}), bf16[32,136,128]{2,1,0:T(8,128)(2,1)S(1)}, u32[]{:S(2)}, u32[]{:S(2)}) async-start(bf16[32,136,128]{2,1,0:T(8,128)(2,1)} %pack_first_groups.1), calls=%async_computation | async-start | bytes 2228224 | tf_op jit(solution)/shard_map/all_to_all | solution.py:747
  10.6 7.8 %collective-permute-start.1 = (bf16[16,2048]{1,0:T(8,128)(2,1)S(1)}, bf16[16,2048]{1,0:T(8,128)(2,1)S(1)}, u32[]{:S(2)}, u32[]{:S(2)}) collective-permute-start(bf16[16,2048]{1,0:T(8,128)(2,1)S(1)} %get-tuple-element.43), channel_id=1, source_target_pairs={{1,0},{2,1},{3,2},{5,4},{6,5},{7,6},{9,8},{10,9},{11,10},{13,12},{... | collective-permute-start | bytes 196616 | tf_op jit(solution)/shard_map/ppermute | solution.py:731
  11.9 6.5 %collective-permute-start = (bf16[16,2048]{1,0:T(8,128)(2,1)S(1)}, bf16[16,2048]{1,0:T(8,128)(2,1)S(1)}, u32[]{:S(2)}, u32[]{:S(2)}) collective-permute-start(bf16[16,2048]{1,0:T(8,128)(2,1)S(1)} %get-tuple-element.42), channel_id=1, source_target_pairs={{0,1},{1,2},{2,3},{4,5},{5,6},{6,7},{8,9},{9,10},{10,11},{12,13},{... | collective-permute-start | bytes 196616 | tf_op jit(solution)/shard_map/ppermute | solution.py:730
  18.3 1.0 copy-start.9
  22.3 3.2 %copy-start = (bf16[7,288,2048]{2,1,0:T(8,128)(2,1)}, bf16[7,288,2048]{2,1,0:T(8,128)(2,1)S(1)}, u32[]{:S(2)}) copy-start(bf16[7,288,2048]{2,1,0:T(8,128)(2,1)S(1)} %column_pass.1.images.source) | copy-start | bytes 24772612
  38.2 75.5 %all-to-all-start.1 = ((bf16[64,16,1536]{2,1,0:T(8,128)(2,1)}), bf16[64,16,1536]{2,1,0:T(8,128)(2,1)}, u32[]{:S(2)}, u32[]{:S(2)}) async-start(bf16[64,16,1536]{2,1,0:T(8,128)(2,1)} %pack_blocks.1), calls=%async_computation.1 | async-start | bytes 6291456 | tf_op jit(solution)/shard_map/all_to_all | solution.py:754
  43.8 5.8 %copy-start.3 = (bf16[512,1024]{1,0:T(8,128)(2,1)}, bf16[512,1024]{1,0:T(8,128)(2,1)S(1)}, u32[]{:S(2)}) copy-start(bf16[512,1024]{1,0:T(8,128)(2,1)S(1)} %get-tuple-element.23.placing) | copy-start | bytes 3145732
  43.8 5.8 %copy-start.5 = (f32[512,128]{1,0:T(8,128)}, f32[512,128]{1,0:T(8,128)S(1)}, u32[]{:S(2)}) copy-start(f32[512,128]{1,0:T(8,128)S(1)} %get-tuple-element.24.factor.factor_hbm) | copy-start | bytes 786436
  43.8 3.8 %copy-start.1 = (bf16[7,288,2048]{2,1,0:T(8,128)(2,1)S(1)}, bf16[7,288,2048]{2,1,0:T(8,128)(2,1)}, u32[]{:S(2)}) copy-start(bf16[7,288,2048]{2,1,0:T(8,128)(2,1)} %copy-done) | copy-start | bytes 24772612
  47.6 3.5 %copy-start.2 = (bf16[7,288,2048]{2,1,0:T(8,128)(2,1)S(1)}, bf16[7,288,2048]{2,1,0:T(8,128)(2,1)}, u32[]{:S(2)}) copy-start(bf16[7,288,2048]{2,1,0:T(8,128)(2,1)} %copy-done) | copy-start | bytes 24772612
  47.6 3.6 %copy-start.10 = (bf16[1792,96]{1,0:T(8,128)(2,1)S(1)}, bf16[1792,96]{1,0:T(8,128)(2,1)}, u32[]{:S(2)}) copy-start(bf16[1792,96]{1,0:T(8,128)(2,1)} %constant.57.clone.table) | copy-start | bytes 1032196
  49.6 0.8 copy-start.7
  50.4 32.1 %copy-start.11 = (f32[128,688]{1,0:T(8,128)}, f32[128,688]{1,0:T(8,128)S(1)}, u32[]{:S(2)}) copy-start(f32[128,688]{1,0:T(8,128)S(1)} %get-tuple-element.28.before_hbm) | copy-start | bytes 1056772
  51.2 62.5 %copy-start.4 = (bf16[512,1024]{1,0:T(8,128)(2,1)S(1)}, bf16[512,1024]{1,0:T(8,128)(2,1)}, u32[]{:S(2)}) copy-start(bf16[512,1024]{1,0:T(8,128)(2,1)} %copy-done.3) | copy-start | bytes 3145732
  98.8 28.1 %copy-start.6 = (f32[7,64,96]{2,1,0:T(8,128)S(1)}, f32[7,64,96]{2,1,0:T(8,128)}, u32[]{:S(2)}) copy-start(f32[7,64,96]{2,1,0:T(8,128)} %constant.58.clone.table_hbm.table) | copy-start | bytes 516100
  113.7 13.3 %copy-start.8 = (bf16[2,256,512]{2,1,0:T(8,128)(2,1)S(1)}, bf16[2,256,512]{2,1,0:T(8,128)(2,1)}, u32[]{:S(2)}) copy-start(bf16[2,256,512]{2,1,0:T(8,128)(2,1)} %copy-done.7) | copy-start | bytes 1572868
